TPU v7x, 32 devices: a whole 2x2x4 slice. The times are simulated.
32 devices in a mesh: group: 2 (over y), ctx: 4 (over z), smp: 2 (over x), head: 2 (over core).
Axes of the slice: x: 2, y: 2, z: 4, core: 2. Of those that a mesh axis runs over, the one named last changes fastest.
Arguments:
- queries: bfloat16 [512, 2, 4096], P(('group', 'smp'), 'head'), parts along dimension 0, may hold values from -8 to 8
- prefix_cache: bfloat16 [2, 8192, 2, 512], P(None, ('group', 'ctx'), 'head'), parts along dimension 1, may hold values from -8 to 8
- suffix_cache: bfloat16 [2, 512, 128, 2, 512], P(None, ('group', 'ctx', 'smp'), None, 'head'), parts along dimension 1, may hold values from -8 to 8
- suffix_length: int32 [512], P(('group', 'smp')), parts along dimension 0, may hold values from 1 to 128, as said below
- cache_sample: int32 [512], P('group'), parts along dimension 0, may hold values from 0 to 255, as said below
- residual: bfloat16 [512, 8192], P(('group', 'ctx', 'head'), 'smp'), parts along dimension 0, may hold values from -6 to 6
- w_out: bfloat16 [2, 4096, 8192], P('head', 'ctx', 'smp'), may hold values from -0.75 to 0.75
- norm_gain: float32 [8192], P('smp'), may hold values from 0.1 to 1.9
- gate_matrix: bfloat16 [8192, 16384], P('smp', ('ctx', 'head')), may hold values from -0.0625 to 0.0625
- w_up: bfloat16 [8192, 16384], P('smp', ('ctx', 'head')), may hold values from -0.0625 to 0.0625
- w_down: bfloat16 [16384, 8192], P(('ctx', 'head'), 'smp'), may hold values from -0.046875 to 0.046875
Outputs:
- mixed: bfloat16 [512, 8192], P(('group', 'ctx', 'head'), 'smp'), parts along dimension 0
There are 2 independent parts, one for each index of `group`. A program takes and returns all parts, laid end to end along the dimension named above; an argument that names none is the same for every part. Nothing has to cross between parts.
Inputs may be any that keep to these rules, and one draw needn't show every extreme that they name: `suffix_length`: the longest is exactly 128 in every draw. A permutation; cache row r and sample cache_sample[r] lie in the same group, the group of row r being (r // 32) % (2) and that of sample i being i // 128.
All inputs are finite; a program needn't handle non-finite values.
Results may differ from a plain program's by a relative error of at most 0.012.
Values may be sent and summed in bfloat16 or wider, within the bound.
A program may use at most 192 MiB of HBM per device.

v0:
```python
import functools

import jax
import jax.numpy as jnp
from jax import lax
from jax.experimental import pallas as pl
from jax.experimental.pallas import tpu as pltpu
from jax.sharding import PartitionSpec as P

D = 8192
QUERY_HEADS = 64
KEY_VALUE_HEADS = 8
HD = 128


EPSILON = 1e-05


def suffix_kernel(lengths_ref, queries_ref, cache_ref, out_ref, lse_ref):
    block, heads, _ = queries_ref.shape
    positions_here, width = cache_ref.shape[2:]
    per_key = heads // (width // HD)
    first = pl.program_id(0) * block
    same = (
        lax.broadcasted_iota(jnp.int32, (heads, width), 0) // per_key
        == lax.broadcasted_iota(jnp.int32, (heads, width), 1) // HD
    )
    positions = lax.broadcasted_iota(jnp.int32, (heads, positions_here), 1)
    for r in range(block):
        q = queries_ref[r].astype(jnp.float32)
        spread = jnp.concatenate([q] * (width // HD), axis=1)
        spread = jnp.where(same, spread, 0.0).astype(jnp.bfloat16)
        scores = lax.dot_general(
            spread, cache_ref[0, r], (((1,), (1,)), ((), ())), preferred_element_type=jnp.float32
        )
        scores = jnp.where(positions < lengths_ref[first + r], scores * HD ** (-0.5), -jnp.inf)
        high = jnp.max(scores, axis=1, keepdims=True)
        weights = jnp.exp(scores - high)
        total = jnp.sum(weights, axis=1, keepdims=True)
        summed = jnp.dot(
            weights.astype(jnp.bfloat16), cache_ref[1, r], preferred_element_type=jnp.float32
        )
        own = jnp.concatenate(
            [
                summed[j * per_key : (j + 1) * per_key, j * HD : (j + 1) * HD]
                for j in range(width // HD)
            ],
            axis=0,
        )
        out_ref[r] = (own / total).astype(jnp.bfloat16)
        lse_ref[r] = high + jnp.log(total)


def suffix_piece(row_queries, suffix_cache, row_lengths):
    rows, heads, _ = row_queries.shape
    block = min(8, rows)
    _, _, positions_here, width = suffix_cache.shape
    return pl.pallas_call(
        suffix_kernel,
        grid=(rows // block,),
        out_shape=(
            jax.ShapeDtypeStruct((rows, heads, HD), jnp.bfloat16),
            jax.ShapeDtypeStruct((rows, heads, 1), jnp.float32),
        ),
        in_specs=[
            pl.BlockSpec(memory_space=pltpu.SMEM),
            pl.BlockSpec((block, heads, HD), lambda i: (i, 0, 0)),
            pl.BlockSpec((2, block, positions_here, width), lambda i: (0, i, 0, 0)),
        ],
        out_specs=(
            pl.BlockSpec((block, heads, HD), lambda i: (i, 0, 0)),
            pl.BlockSpec((block, heads, 1), lambda i: (i, 0, 0)),
        ),
        compiler_params=pltpu.CompilerParams(vmem_limit_bytes=57 * 1024 * 1024),
    )(row_lengths, row_queries, suffix_cache)


MESH = pl.DeviceIdType.MESH
TILE = 512
VMEM_BYTES = 62 * 1024 * 1024


def remote(src, dst, send_sem, recv_sem, where):
    return pltpu.make_async_remote_copy(
        src_ref=src,
        dst_ref=dst,
        send_sem=send_sem,
        recv_sem=recv_sem,
        device_id=where,
        device_id_type=MESH,
    )


def greet(n, n_smp, c, s, h):
    barrier = pltpu.get_barrier_semaphore()
    for k in range(1, n):
        pl.semaphore_signal(barrier, inc=1, device_id={"ctx": lax.rem(c + k, n)}, device_id_type=MESH)
    for k in range(1, n_smp):
        pl.semaphore_signal(
            barrier, inc=1, device_id={"smp": lax.rem(s + k, n_smp)}, device_id_type=MESH
        )
    pl.semaphore_signal(barrier, inc=1, device_id={"head": 1 - h}, device_id_type=MESH)
    pl.semaphore_wait(barrier, (n - 1) + (n_smp - 1) + 1)


class Line:
    def __init__(self, n, c, h, buf_a, recv_a, buf_b, from_left, from_right, sa, ra, ss, rl, rr):
        self.n, self.c, self.h = n, c, h
        self.buf_a, self.recv_a, self.buf_b = buf_a, recv_a, buf_b
        self.from_left, self.from_right = from_left, from_right
        self.sa, self.ra, self.ss, self.rl, self.rr = sa, ra, ss, rl, rr
        self.tiles = buf_a.shape[0]

        @pl.when(c == 0)
        def _():
            from_left[:, 0] = jnp.zeros(from_left.shape[:1] + from_left.shape[2:], from_left.dtype)

        @pl.when(c == n - 1)
        def _():
            from_right[:, n - 1] = jnp.zeros(
                from_right.shape[:1] + from_right.shape[2:], from_right.dtype
            )

    def pair_copy(self, t):
        return remote(
            self.buf_a.at[t, 1 - self.h],
            self.recv_a.at[t],
            self.sa.at[t],
            self.ra.at[t],
            {"head": 1 - self.h},
        )

    def to_right(self, t, d):
        return remote(
            self.buf_b.at[t, d],
            self.from_left.at[t, d],
            self.ss.at[t, d],
            self.rl.at[t, d],
            {"ctx": lax.rem(self.c + 1, self.n)},
        )

    def to_left(self, t, d):
        return remote(
            self.buf_b.at[t, d],
            self.from_right.at[t, d],
            self.ss.at[t, d],
            self.rr.at[t, d],
            {"ctx": lax.rem(self.c + self.n - 1, self.n)},
        )

    def give(self, t, value):
        _, _, n, rows, width = self.buf_a.shape
        parts = value.reshape(n, 2, rows, width).astype(jnp.bfloat16)
        self.buf_a[t, 0] = parts[:, 0]
        self.buf_a[t, 1] = parts[:, 1]
        self.pair_copy(t).start()

    def middle(self, t):
        self.pair_copy(t).wait()
        both = self.buf_a[t, self.h].astype(jnp.float32) + self.recv_a[t].astype(jnp.float32)
        self.buf_b[t] = both.astype(jnp.bfloat16)

    def hop(self, t, inside, d, copy_of, arrived, first):
        @pl.when(inside & (t >= 0) & (t < self.tiles))
        def _():
            @pl.when(jnp.logical_not(first))
            def _():
                copy_of(t, d).wait_recv()
                both = self.buf_b[t, d].astype(jnp.float32) + arrived[t, d].astype(jnp.float32)
                self.buf_b[t, d] = both.astype(jnp.bfloat16)

            copy_of(t, d).start()

    def step(self, i):
        n, c = self.n, self.c

        @pl.when((i >= 1) & (i <= self.tiles))
        def _():
            self.middle(i - 1)

        for e in range(n - 1):
            right, left = n - 1 - e, e
            self.hop(i - 1 - c, right > c, right, self.to_right, self.from_left, c == 0)
            self.hop(i - n + c, left < c, left, self.to_left, self.from_right, c == n - 1)

    def finish(self, t):
        n, c = self.n, self.c

        @pl.when(c > 0)
        def _():
            self.to_right(t, c).wait_recv()

        @pl.when(c < n - 1)
        def _():
            self.to_left(t, c).wait_recv()

        return (
            self.buf_b[t, c].astype(jnp.float32)
            + self.from_left[t, c].astype(jnp.float32)
            + self.from_right[t, c].astype(jnp.float32)
        )

    def drain(self, t):
        for d in range(self.n):

            @pl.when(d > self.c)
            def _():
                self.to_right(t, d).wait_send()

            @pl.when(d < self.c)
            def _():
                self.to_left(t, d).wait_send()


class Scatter:
    def __init__(self, n, c, h, buf_a, recv_a, buf_b, recv_b, sa, ra, sb, rb):
        self.n, self.c, self.h = n, c, h
        self.buf_a, self.recv_a, self.buf_b, self.recv_b = buf_a, recv_a, buf_b, recv_b
        self.sa, self.ra, self.sb, self.rb = sa, ra, sb, rb

    def pair_copy(self, t):
        return remote(
            self.buf_a.at[t, 1 - self.h],
            self.recv_a.at[t],
            self.sa.at[t],
            self.ra.at[t],
            {"head": 1 - self.h},
        )

    def row_copy(self, t, k):
        d = lax.rem(self.c + k, self.n)
        return remote(
            self.buf_b.at[t, d],
            self.recv_b.at[t, k - 1],
            self.sb.at[t, k - 1],
            self.rb.at[t, k - 1],
            {"ctx": d},
        )

    def give(self, t, value):
        _, _, n, rows, width = self.buf_a.shape
        parts = value.reshape(n, 2, rows, width).astype(jnp.bfloat16)
        self.buf_a[t, 0] = parts[:, 0]
        self.buf_a[t, 1] = parts[:, 1]
        self.pair_copy(t).start()

    def middle(self, t):
        self.pair_copy(t).wait()
        both = self.buf_a[t, self.h].astype(jnp.float32) + self.recv_a[t].astype(jnp.float32)
        self.buf_b[t] = both.astype(jnp.bfloat16)
        for k in range(1, self.n):
            self.row_copy(t, k).start()

    def finish(self, t):
        total = self.buf_b[t, self.c].astype(jnp.float32)
        for k in range(1, self.n):
            self.row_copy(t, k).wait()
            total = total + self.recv_b[t, k - 1].astype(jnp.float32)
        return total


def columns(t, width):
    return pl.ds(pl.multiple_of(t * width, width), width)


def proj_kernel(
    n,
    n_smp,
    q_ref,
    kv_ref,
    suf_ref,
    suf_lse_ref,
    w_ref,
    res_ref,
    state_ref,
    out_mine,
    lse_mine,
    out_in,
    lse_in,
    attn,
    w_buf,
    buf_a,
    recv_a,
    buf_b,
    from_left,
    from_right,
    w_sem,
    os,
    orr,
    ls,
    lr,
    xs,
    xr,
    sa,
    ra,
    ss,
    rl,
    rr,
    gsr,
    gsl,
    gr,
    fs,
    fr,
):
    c, s, h = lax.axis_index("ctx"), lax.axis_index("smp"), lax.axis_index("head")
    tiles = w_buf.shape[0]
    keys, samples, per_key = suf_lse_ref.shape
    per_dest = out_mine.shape[2] // HD
    dests = per_key // per_dest
    together = 4

    greet(n, n_smp, c, s, h)

    def piece_copies(at, d):
        return (
            remote(out_mine.at[d], out_in.at[at], os.at[d], orr.at[at], {"ctx": d}),
            remote(lse_mine.at[d], lse_in.at[at], ls.at[d], lr.at[at], {"ctx": d}),
        )

    def w_copy(t):
        return pltpu.make_async_copy(w_ref.at[:, columns(t, TILE)], w_buf.at[t], w_sem.at[t])

    @pl.loop(0, tiles)
    def _(t):
        w_copy(t).start()

    lanes_at = lax.broadcasted_iota(jnp.int32, (samples, 128), 1)

    @pl.loop(0, keys)
    def _(i):
        j = lax.rem(lax.div(c, dests) + 1 + i, keys)
        key = kv_ref[0, :, columns(j, HD)]
        value = kv_ref[1, :, columns(j, HD)]
        own = q_ref[:, columns(j, per_key * HD)]
        placed = suf_ref[:, columns(j, per_key * HD)]
        placed_lse = suf_lse_ref[j]
        tables = [jnp.zeros((samples, 128), jnp.float32) for _ in range(dests)]
        for g0 in range(0, per_key, together):
            rows = jnp.concatenate(
                [own[:, g * HD : (g + 1) * HD] for g in range(g0, g0 + together)], axis=0
            )
            scores = lax.dot_general(
                rows, key, (((1,), (1,)), ((), ())), preferred_element_type=jnp.float32
            ) * HD ** (-0.5)
            high = jnp.max(scores, axis=1, keepdims=True)
            weights = jnp.exp(scores - high)
            total = jnp.sum(weights, axis=1, keepdims=True)
            summed = (
                jnp.dot(weights.astype(jnp.bfloat16), value, preferred_element_type=jnp.float32)
                / total
            )
            lse = high + jnp.log(total)
            for g in range(g0, g0 + together):
                part = slice((g - g0) * samples, (g - g0 + 1) * samples)
                own_lse, other_lse = lse[part], placed_lse[:, g : g + 1]
                top = jnp.maximum(own_lse, other_lse)
                own_weight = jnp.exp(own_lse - top)
                other_weight = jnp.exp(other_lse - top)
                both = own_weight + other_weight
                merged = (
                    own_weight * summed[part]
                    + other_weight * placed[:, g * HD : (g + 1) * HD].astype(jnp.float32)
                ) / both
                at = g % per_dest
                out_mine[j * dests + g // per_dest, :, at * HD : (at + 1) * HD] = merged.astype(
                    jnp.bfloat16
                )
                q = g // per_dest
                tables[q] = jnp.where(lanes_at == at, top + jnp.log(both), tables[q])
        for q in range(dests):
            d = j * dests + q
            lse_mine[d] = tables[q].T[:8]

            @pl.when(d != c)
            def _():
                for copy in piece_copies(c, d):
                    copy.start()

    for k in range(1, n):
        d = lax.rem(c + k, n)
        for copy in piece_copies(d, d):
            copy.wait_recv()
    for k in range(1, n):
        d = lax.rem(c + k, n)
        for copy in piece_copies(c, d):
            copy.wait_send()

    lses = [lse_mine[c]] + [lse_in[lax.rem(c + k, n)] for k in range(1, n)]
    peak = functools.reduce(jnp.maximum, lses)
    scales = [jnp.exp(value - peak) for value in lses]
    denom = functools.reduce(jnp.add, scales)
    blank = jnp.zeros((120, samples), jnp.float32)
    scales = [jnp.concatenate([value / denom, blank], axis=0).T for value in scales]
    for j in range(per_dest):
        lanes = slice(j * HD, (j + 1) * HD)
        total = scales[0][:, j : j + 1] * out_mine[c, :, lanes].astype(jnp.float32)
        for k in range(1, n):
            piece = out_in[lax.rem(c + k, n), :, lanes].astype(jnp.float32)
            total = total + scales[k][:, j : j + 1] * piece
        attn[s, :, lanes] = total.astype(jnp.bfloat16)

    def attn_copy(k):
        return remote(
            attn.at[s], attn.at[s], xs.at[k - 1], xr.at[k - 1], {"smp": lax.rem(s + k, n_smp)}
        )

    for k in range(1, n_smp):
        attn_copy(k).start()
    for k in range(1, n_smp):
        attn_copy(k).wait()

    line = Line(n, c, h, buf_a, recv_a, buf_b, from_left, from_right, sa, ra, ss, rl, rr)

    def gather_copy(t, q, way, sems):
        block = state_ref.at[q, h, :, columns(t, TILE)]
        return remote(
            block, block, sems.at[t, q], gr.at[t, q], {"ctx": lax.rem(c + way, n)}
        )

    def pass_copy(t, q):
        block = state_ref.at[q, h, :, columns(t, TILE)]
        return remote(block, block, fs.at[t, q], fr.at[t, q], {"head": 1 - h})

    def spread(t, q, right, left):
        @pl.when(right & (c < n - 1))
        def _():
            gather_copy(t, q, 1, gsr).start()

        @pl.when(left & (c > 0))
        def _():
            gather_copy(t, q, n - 1, gsl).start()

        pass_copy(t, q).start()

    @pl.loop(0, tiles + 2 * n - 1)
    def _(i):
        @pl.when(i < tiles)
        def _():
            w_copy(i).wait()
            rows = attn[...].reshape(-1, attn.shape[2])
            line.give(i, jnp.dot(rows, w_buf[i], preferred_element_type=jnp.float32))

        line.step(i)

        @pl.when((i >= n) & (i < tiles + n))
        def _():
            t = i - n
            own = line.finish(t) + res_ref[:, columns(t, TILE)].astype(jnp.float32)
            state_ref[c, h, :, columns(t, TILE)] = own.astype(jnp.bfloat16)
            spread(t, c, c >= 0, c >= 0)

        for q in range(n):
            t = i - n - lax.max(c - q, q - c)

            @pl.when((q != c) & (t >= 0) & (t < tiles))
            def _():
                gather_copy(t, q, 1, gsr).wait_recv()
                spread(t, q, q < c, q > c)

    @pl.loop(0, tiles)
    def _(t):
        line.drain(t)
        for q in range(n):

            @pl.when((q <= c) & (c < n - 1))
            def _():
                gather_copy(t, q, 1, gsr).wait_send()

            @pl.when((q >= c) & (c > 0))
            def _():
                gather_copy(t, q, n - 1, gsl).wait_send()

            pass_copy(t, q).wait()


def project(n, n_smp, queries, prefix_cache, suffix_out, suffix_lse, w, residual):
    keys, samples, per_key = suffix_lse.shape
    features = queries.shape[1] // n
    rows, width = residual.shape
    tiles = width // TILE
    vmem = pl.BlockSpec(memory_space=pltpu.VMEM)
    dma = pltpu.SemaphoreType.DMA
    bf16 = jnp.bfloat16
    return pl.pallas_call(
        functools.partial(proj_kernel, n, n_smp),
        out_shape=jax.ShapeDtypeStruct((n, 2, rows, width), bf16),
        in_specs=[vmem, vmem, vmem, vmem, pl.BlockSpec(memory_space=pl.ANY), vmem],
        out_specs=vmem,
        scratch_shapes=[
            pltpu.VMEM((n, samples, features), bf16),
            pltpu.VMEM((n, 8, samples), jnp.float32),
            pltpu.VMEM((n, samples, features), bf16),
            pltpu.VMEM((n, 8, samples), jnp.float32),
            pltpu.VMEM((n_smp, samples, features), bf16),
            pltpu.VMEM((tiles, w.shape[0], TILE), bf16),
            pltpu.VMEM((tiles, 2, n, rows, TILE), bf16),
            pltpu.VMEM((tiles, n, rows, TILE), bf16),
            pltpu.VMEM((tiles, n, rows, TILE), bf16),
            pltpu.VMEM((tiles, n, rows, TILE), bf16),
            pltpu.VMEM((tiles, n, rows, TILE), bf16),
            dma((tiles,)),
            dma((n,)),
            dma((n,)),
            dma((n,)),
            dma((n,)),
            dma((n_smp - 1,)),
            dma((n_smp - 1,)),
            dma((tiles,)),
            dma((tiles,)),
            dma((tiles, n)),
            dma((tiles, n)),
            dma((tiles, n)),
            dma((tiles, n)),
            dma((tiles, n)),
            dma((tiles, n)),
            dma((tiles, n)),
            dma((tiles, n)),
        ],
        compiler_params=pltpu.CompilerParams(
            collective_id=0, has_side_effects=True, vmem_limit_bytes=VMEM_BYTES
        ),
    )(queries, prefix_cache, suffix_out, suffix_lse, w, residual)


UNITS = 256
SLOTS = 4


def ffn_kernel(
    n,
    n_smp,
    state_ref,
    gain_ref,
    gate_ref,
    up_ref,
    down_ref,
    mixed_ref,
    scaled,
    squares,
    squares_in,
    gate_buf,
    up_buf,
    down_buf,
    part,
    part_in,
    hidden,
    buf_a,
    recv_a,
    buf_b,
    recv_b,
    g_sem,
    u_sem,
    d_sem,
    qs,
    qr,
    ps,
    pr,
    hs,
    hr,
    sa,
    ra,
    sb,
    rb,
):
    c, s, h = lax.axis_index("ctx"), lax.axis_index("smp"), lax.axis_index("head")
    steps = part.shape[0]
    slots = gate_buf.shape[0]
    tiles = down_buf.shape[0]
    width = state_ref.shape[3]
    all_rows = state_ref.shape[0] * 2 * state_ref.shape[2]
    smp_rows = all_rows // n_smp

    def weight_copies(t):
        slot = lax.rem(t, slots)
        return (
            pltpu.make_async_copy(
                gate_ref.at[:, columns(t, UNITS)], gate_buf.at[slot], g_sem.at[slot]
            ),
            pltpu.make_async_copy(up_ref.at[:, columns(t, UNITS)], up_buf.at[slot], u_sem.at[slot]),
        )

    def down_copy(t):
        return pltpu.make_async_copy(down_ref.at[:, columns(t, TILE)], down_buf.at[t], d_sem.at[t])

    @pl.loop(0, min(slots, steps))
    def _(t):
        for copy in weight_copies(t):
            copy.start()

    greet(n, n_smp, c, s, h)

    for block in range(n):
        wide = state_ref[block].reshape(-1, width).astype(jnp.float32)
        rows = slice(block * wide.shape[0], (block + 1) * wide.shape[0])
        scaled[rows] = (wide * gain_ref[...]).astype(jnp.bfloat16)
        sums = jnp.sum(wide * wide, axis=1, keepdims=True)
        squares[rows] = jnp.broadcast_to(sums, (wide.shape[0], 128))

    def smp_rows_of(p):
        return pl.ds(pl.multiple_of(p * smp_rows, smp_rows), smp_rows)

    def square_copy(k):
        p = lax.rem(s + k, n_smp)
        return remote(
            squares.at[smp_rows_of(p)], squares_in.at[k - 1], qs.at[k - 1], qr.at[k - 1], {"smp": p}
        )

    for k in range(1, n_smp):
        square_copy(k).start()

    def part_copy(t, k):
        p = lax.rem(s + k, n_smp)
        return remote(
            part.at[t, smp_rows_of(p)],
            part_in.at[t, k - 1],
            ps.at[t, k - 1],
            pr.at[t, k - 1],
            {"smp": p},
        )

    def hidden_copy(t, k):
        block = hidden.at[smp_rows_of(s), columns(t, UNITS)]
        return remote(
            block, block, hs.at[t, k - 1], hr.at[t, k - 1], {"smp": lax.rem(s + k, n_smp)}
        )

    def act(t):
        both = part[t, smp_rows_of(s)].astype(jnp.float32)
        for k in range(1, n_smp):
            part_copy(t, k).wait()
            both = both + part_in[t, k - 1].astype(jnp.float32)
        total = squares[smp_rows_of(s)]
        for k in range(1, n_smp):
            total = total + squares_in[k - 1]
        factor = lax.rsqrt(total / (width * n_smp) + EPSILON)[:, :1]
        gate = factor * both[:, :UNITS]
        up = factor * both[:, UNITS:]
        value = gate / (1.0 + jnp.exp(-gate)) * up
        hidden[smp_rows_of(s), columns(t, UNITS)] = value.astype(jnp.bfloat16)
        for k in range(1, n_smp):
            hidden_copy(t, k).start()

    lag = min(2, steps)

    @pl.loop(0, steps)
    def _(t):
        for copy in weight_copies(t):
            copy.wait()
        slot = lax.rem(t, slots)
        part[t, :, :UNITS] = jnp.dot(
            scaled[...], gate_buf[slot], preferred_element_type=jnp.float32
        ).astype(jnp.bfloat16)
        part[t, :, UNITS:] = jnp.dot(
            scaled[...], up_buf[slot], preferred_element_type=jnp.float32
        ).astype(jnp.bfloat16)
        for k in range(1, n_smp):
            part_copy(t, k).start()

        @pl.when(t + slots < steps)
        def _():
            for copy in weight_copies(t + slots):
                copy.start()

        @pl.when(t < tiles)
        def _():
            down_copy(t).start()

        @pl.when(t == lag)
        def _():
            for k in range(1, n_smp):
                square_copy(k).wait()

        @pl.when(t >= lag)
        def _():
            act(t - lag)

    if steps <= lag:
        for k in range(1, n_smp):
            square_copy(k).wait()

    for t in range(steps, tiles):
        down_copy(t).start()

    @pl.loop(steps - lag, steps)
    def _(t):
        act(t)

    @pl.loop(0, steps)
    def _(t):
        for k in range(1, n_smp):
            hidden_copy(t, k).wait()

    scatter = Scatter(n, c, h, buf_a, recv_a, buf_b, recv_b, sa, ra, sb, rb)

    @pl.loop(0, tiles)
    def _(t):
        down_copy(t).wait()
        scatter.give(t, jnp.dot(hidden[...], down_buf[t], preferred_element_type=jnp.float32))

        @pl.when(t >= 1)
        def _():
            scatter.middle(t - 1)

    scatter.middle(tiles - 1)

    @pl.loop(0, tiles)
    def _(t):
        own = scatter.finish(t) + state_ref[c, h, :, columns(t, TILE)].astype(jnp.float32)
        mixed_ref[:, columns(t, TILE)] = own.astype(jnp.bfloat16)


def feed_forward(n, n_smp, state, gain, gate, up, down):
    _, _, rows, width = state.shape
    all_rows = n * 2 * rows
    smp_rows = all_rows // n_smp
    units = gate.shape[1]
    steps, tiles = units // UNITS, width // TILE
    slots = min(SLOTS, steps)
    vmem = pl.BlockSpec(memory_space=pltpu.VMEM)
    hbm = pl.BlockSpec(memory_space=pl.ANY)
    dma = pltpu.SemaphoreType.DMA
    bf16 = jnp.bfloat16
    return pl.pallas_call(
        functools.partial(ffn_kernel, n, n_smp),
        out_shape=jax.ShapeDtypeStruct((rows, width), bf16),
        in_specs=[vmem, vmem, hbm, hbm, hbm],
        out_specs=vmem,
        scratch_shapes=[
            pltpu.VMEM((all_rows, width), bf16),
            pltpu.VMEM((all_rows, 128), jnp.float32),
            pltpu.VMEM((n_smp - 1, smp_rows, 128), jnp.float32),
            pltpu.VMEM((slots, width, UNITS), bf16),
            pltpu.VMEM((slots, width, UNITS), bf16),
            pltpu.VMEM((tiles, units, TILE), bf16),
            pltpu.VMEM((steps, all_rows, 2 * UNITS), bf16),
            pltpu.VMEM((steps, n_smp - 1, smp_rows, 2 * UNITS), bf16),
            pltpu.VMEM((all_rows, units), bf16),
            pltpu.VMEM((tiles, 2, n, rows, TILE), bf16),
            pltpu.VMEM((tiles, n, rows, TILE), bf16),
            pltpu.VMEM((tiles, n, rows, TILE), bf16),
            pltpu.VMEM((tiles, n - 1, rows, TILE), bf16),
            dma((slots,)),
            dma((slots,)),
            dma((tiles,)),
            dma((n_smp - 1,)),
            dma((n_smp - 1,)),
            dma((steps, n_smp - 1)),
            dma((steps, n_smp - 1)),
            dma((steps, n_smp - 1)),
            dma((steps, n_smp - 1)),
            dma((tiles,)),
            dma((tiles,)),
            dma((tiles, n - 1)),
            dma((tiles, n - 1)),
        ],
        compiler_params=pltpu.CompilerParams(
            collective_id=1, has_side_effects=True, vmem_limit_bytes=VMEM_BYTES
        ),
    )(state, gain, gate, up, down)


def on_device(
    queries,
    prefix_cache,
    suffix_cache,
    suffix_length,
    cache_sample,
    residual,
    w_out,
    norm_gain,
    gate_matrix,
    w_up,
    w_down,
):
    group_rows = queries.shape[0]
    keys_here = prefix_cache.shape[3] // HD
    heads_local = queries.shape[2] // HD
    n, n_smp = lax.axis_size("ctx"), lax.axis_size("smp")
    own_queries = queries[:, 0]
    rows_here = suffix_cache.shape[1]
    flat_index = lax.axis_index("ctx") * n_smp + lax.axis_index("smp")
    row_ids = lax.dynamic_slice_in_dim(cache_sample, flat_index * rows_here, rows_here, 0)
    local_ids = row_ids % group_rows
    row_queries = jnp.take(own_queries, local_ids, axis=0).reshape(rows_here, heads_local, HD)
    row_lengths = jnp.take(suffix_length, local_ids, axis=0)
    suffix_out, suffix_lse = suffix_piece(row_queries, suffix_cache[:, :, :, 0], row_lengths)
    chosen = local_ids[None, :] == jnp.arange(group_rows, dtype=jnp.int32)[:, None]
    placed_out = jnp.dot(
        chosen.astype(jnp.bfloat16),
        suffix_out.reshape(rows_here, -1),
        preferred_element_type=jnp.float32,
    ).astype(jnp.bfloat16)
    placed_lse = jnp.dot(
        chosen.astype(jnp.float32), suffix_lse[:, :, 0], precision=lax.Precision.HIGHEST
    )
    placed_lse = jnp.where(jnp.any(chosen, axis=1)[:, None], placed_lse, -1e30)
    placed_lse = placed_lse.reshape(group_rows, keys_here, -1).transpose(1, 0, 2)
    state = project(
        n,
        n_smp,
        own_queries,
        prefix_cache[:, :, 0],
        placed_out,
        placed_lse,
        w_out[0],
        residual,
    )
    return feed_forward(n, n_smp, state, norm_gain[None, :], gate_matrix, w_up, w_down)


def solution(mesh):
    in_specs = (
        P(("group", "smp"), "head", None),
        P(None, ("group", "ctx"), "head", None),
        P(None, ("group", "ctx", "smp"), None, "head", None),
        P(("group", "smp")),
        P("group"),
        P(("group", "ctx", "head"), "smp"),
        P("head", "ctx", "smp"),
        P("smp"),
        P("smp", ("ctx", "head")),
        P("smp", ("ctx", "head")),
        P(("ctx", "head"), "smp"),
    )
    out_specs = P(("group", "ctx", "head"), "smp")
    return jax.shard_map(
        on_device, mesh=mesh, in_specs=in_specs, out_specs=out_specs, check_vma=False
    )
```

profile of v0, /device:TPU:0, one launch (start us, length us, event | category | flops | bytes accessed | tf_op | source)
XLA Modules:
  0.0 178.2 jit_solution(13672538014682459026)
XLA Ops:
  0.0 0.0 copy-start
  0.0 0.8 compare_select_fusion
  0.8 0.1 fusion.3
  0.9 0.0 copy-done
  0.9 0.7 gather_fusion
  1.6 0.6 broadcast_select_fusion
  2.2 2.3 %gather_fusion.1 = bf16[32,4096]{1,0:T(8,128)(2,1)S(1)} fusion(bf16[128,4096]{1,0:T(8,128)(2,1)} %bitcast.16, s32[1024]{0:T(1024)S(1)} %pad_clamp_fusion), kind=kCustom, calls=%fused_computation.1 | custom fusion | bytes 524416 | tf_op jit(solution)/shard_map/jit(_take)/gather | solution.py:784
  4.5 0.8 bitcast_select_fusion.queries_ref
  5.3 12.0 %shard_map.109 = (bf16[32,32,128]{2,1,0:T(8,128)(2,1)}, f32[32,32,1]{2,1,0:T(8,128)}) custom-call(s32[32]{0:T(128)} %get-tuple-element.9.lengths_ref, bf16[32,32,128]{2,1,0:T(8,128)(2,1)} %bitcast_select_fusion.queries_ref, bf16[2,32,128,512]{3,2,1,0:T(8,128)(2,1)} %bitcast.18), custom_call_target="tpu_custom_call" | custom-call | tf_op jit(solution)/shard_map/pallas_call | solution.py:58
  17.3 1.2 reduce
  18.6 0.2 fusion
  18.8 0.9 copy.13
  19.6 2.5 %convolution_convert_fusion.suf_ref = bf16[128,4096]{1,0:T(8,128)(2,1)} fusion(bf16[4,8,32,128]{3,2,1,0:T(8,128)(2,1)} %bitcast.23, s32[32]{0:T(128)S(1)} %get-tuple-element.12), kind=kOutput, calls=%fused_computation.2 | convolution fusion | flops 34082816 | bytes 1310848 | tf_op jit(solution)/shard_map/dot_general | solution.py:788
  22.1 85.5 %shard_map.110.state_ref = bf16[4,2,32,4096]{3,2,1,0:T(8,128)(2,1)} custom-call(bf16[128,4096]{1,0:T(8,128)(2,1)} %bitcast.17, bf16[2,1024,512]{2,1,0:T(8,128)(2,1)} %bitcast.20, bf16[128,4096]{1,0:T(8,128)(2,1)} %convolution_convert_fusion.suf_ref, f32[4,128,8]{2,1,0:T(8,128)} %bitcast.22, bf16[1024,4096]{1,0:T(8,128)(2,1)} %bitcast.19, ...), custom_call_target="tpu_custom_call" | custom-call | tf_op jit(solution)/shard_map/pallas_call | solution.py:484
  107.6 0.0 copy-start.1
  107.6 68.9 %shard_map.111 = bf16[32,4096]{1,0:T(8,128)(2,1)} custom-call(bf16[4,2,32,4096]{3,2,1,0:T(8,128)(2,1)} %shard_map.110.state_ref, f32[1,4096]{1,0:T(1,128)} %bitcast.24, bf16[4096,2048]{1,0:T(8,128)(2,1)} %gate_ref.1, bf16[4096,2048]{1,0:T(8,128)(2,1)} %up_ref.1, bf16[2048,4096]{1,0:T(8,128)(2,1)} %down_ref.1), custom_call_target="tpu_custom_call" | custom-call | tf_op jit(solution)/shard_map/pallas_call | solution.py:723
  176.5 1.7 copy.21
  178.2 0.0 copy-done.1
  (2 shorter events, 0.0 us)
Async XLA Ops:
  0.0 0.9 copy-start
  107.6 70.6 %copy-start.1 = (s32[128]{0:T(128)S(1)}, s32[128]{0:T(128)}, u32[]{:S(2)}) copy-start(s32[128]{0:T(128)} %param.14) | copy-start | bytes 1540
where the time goes:
time: 179 us; the launch traced here: 178 us
  Pallas kernels  166 us (93%)
  local copies, waits for them, and re-layouts  5.59 us (3%)
  other arithmetic  3.52 us (2%)
  matrix products  2.69 us (2%)
    pallas_call x1, Pallas kernels, project(): pl.pallas_call(functools.partial(proj_kernel, n, n_smp), out_shape=jax.Sh...  85.5 us
    pallas_call x1, Pallas kernels, feed_forward(): pl.pallas_call(functools.partial(ffn_kernel, n, n_smp), out_shape=jax.Sha...  68.9 us
    pallas_call x1, Pallas kernels, suffix_piece(): pl.pallas_call(suffix_kernel, grid=(rows // block,), out_shape=(jax.Shape...  12 us

commit v1 on v0

--- a/solution.py
+++ b/solution.py
@@ -524,6 +524,8 @@
 
 UNITS = 256
 SLOTS = 4
+DOWN_TILE = 1024
+SUB = 16
 
 
 def ffn_kernel(
@@ -547,7 +549,8 @@
     buf_a,
     recv_a,
     buf_b,
-    recv_b,
+    from_left,
+    from_right,
     g_sem,
     u_sem,
     d_sem,
@@ -559,19 +562,22 @@
     hr,
     sa,
     ra,
-    sb,
-    rb,
+    ss,
+    rl,
+    rr,
 ):
     c, s, h = lax.axis_index("ctx"), lax.axis_index("smp"), lax.axis_index("head")
-    steps = part.shape[0]
-    slots = gate_buf.shape[0]
-    tiles = down_buf.shape[0]
-    width = state_ref.shape[3]
-    all_rows = state_ref.shape[0] * 2 * state_ref.shape[2]
-    smp_rows = all_rows // n_smp
-
-    def weight_copies(t):
-        slot = lax.rem(t, slots)
+    slots, width, _ = gate_buf.shape
+    tiles, units, down_tile = down_buf.shape
+    subsets, sub_rows, _ = scaled.shape
+    sub = state_ref.shape[2] // subsets
+    smp_rows = sub_rows // n_smp
+    steps = units // UNITS
+    all_steps, all_tiles = subsets * steps, subsets * tiles
+    ratio = max(1, steps // tiles)
+
+    def weight_copies(i):
+        slot, t = lax.rem(i, slots), lax.rem(i, steps)
         return (
             pltpu.make_async_copy(
                 gate_ref.at[:, columns(t, UNITS)], gate_buf.at[slot], g_sem.at[slot]
@@ -580,142 +586,179 @@
         )
 
     def down_copy(t):
-        return pltpu.make_async_copy(down_ref.at[:, columns(t, TILE)], down_buf.at[t], d_sem.at[t])
-
-    @pl.loop(0, min(slots, steps))
+        return pltpu.make_async_copy(
+            down_ref.at[:, columns(t, down_tile)], down_buf.at[t], d_sem.at[t]
+        )
+
+    @pl.loop(0, min(slots, all_steps))
     def _(t):
         for copy in weight_copies(t):
             copy.start()
 
     greet(n, n_smp, c, s, h)
 
-    for block in range(n):
-        wide = state_ref[block].reshape(-1, width).astype(jnp.float32)
-        rows = slice(block * wide.shape[0], (block + 1) * wide.shape[0])
-        scaled[rows] = (wide * gain_ref[...]).astype(jnp.bfloat16)
-        sums = jnp.sum(wide * wide, axis=1, keepdims=True)
-        squares[rows] = jnp.broadcast_to(sums, (wide.shape[0], 128))
-
     def smp_rows_of(p):
         return pl.ds(pl.multiple_of(p * smp_rows, smp_rows), smp_rows)
 
-    def square_copy(k):
-        p = lax.rem(s + k, n_smp)
-        return remote(
-            squares.at[smp_rows_of(p)], squares_in.at[k - 1], qs.at[k - 1], qr.at[k - 1], {"smp": p}
-        )
-
-    for k in range(1, n_smp):
-        square_copy(k).start()
-
-    def part_copy(t, k):
-        p = lax.rem(s + k, n_smp)
-        return remote(
-            part.at[t, smp_rows_of(p)],
-            part_in.at[t, k - 1],
-            ps.at[t, k - 1],
-            pr.at[t, k - 1],
+    def square_copy(k, m):
+        p = lax.rem(s + m, n_smp)
+        return remote(
+            squares.at[k, smp_rows_of(p)],
+            squares_in.at[k, m - 1],
+            qs.at[k, m - 1],
+            qr.at[k, m - 1],
             {"smp": p},
         )
 
-    def hidden_copy(t, k):
-        block = hidden.at[smp_rows_of(s), columns(t, UNITS)]
-        return remote(
-            block, block, hs.at[t, k - 1], hr.at[t, k - 1], {"smp": lax.rem(s + k, n_smp)}
-        )
-
-    def act(t):
-        both = part[t, smp_rows_of(s)].astype(jnp.float32)
-        for k in range(1, n_smp):
-            part_copy(t, k).wait()
-            both = both + part_in[t, k - 1].astype(jnp.float32)
-        total = squares[smp_rows_of(s)]
-        for k in range(1, n_smp):
-            total = total + squares_in[k - 1]
+    def prepare(k):
+        own = pl.ds(pl.multiple_of(k * sub, sub), sub)
+        for block in range(n):
+            for core in range(2):
+                wide = state_ref[block, core, own].astype(jnp.float32)
+                first = (2 * block + core) * sub
+                rows = slice(first, first + sub)
+                scaled[k, rows] = (wide * gain_ref[...]).astype(jnp.bfloat16)
+                sums = jnp.sum(wide * wide, axis=1, keepdims=True)
+                squares[k, rows] = jnp.broadcast_to(sums, (sub, 128))
+        for m in range(1, n_smp):
+            square_copy(k, m).start()
+
+    def part_copy(i, m):
+        p = lax.rem(s + m, n_smp)
+        return remote(
+            part.at[i, smp_rows_of(p)],
+            part_in.at[i, m - 1],
+            ps.at[i, m - 1],
+            pr.at[i, m - 1],
+            {"smp": p},
+        )
+
+    def hidden_copy(i, m):
+        k, t = lax.div(i, steps), lax.rem(i, steps)
+        block = hidden.at[k, smp_rows_of(s), columns(t, UNITS)]
+        return remote(
+            block, block, hs.at[i, m - 1], hr.at[i, m - 1], {"smp": lax.rem(s + m, n_smp)}
+        )
+
+    def act(i):
+        k, t = lax.div(i, steps), lax.rem(i, steps)
+
+        @pl.when(t == 0)
+        def _():
+            for m in range(1, n_smp):
+                square_copy(k, m).wait()
+
+        both = part[i, smp_rows_of(s)].astype(jnp.float32)
+        for m in range(1, n_smp):
+            part_copy(i, m).wait()
+            both = both + part_in[i, m - 1].astype(jnp.float32)
+        total = squares[k, smp_rows_of(s)]
+        for m in range(1, n_smp):
+            total = total + squares_in[k, m - 1]
         factor = lax.rsqrt(total / (width * n_smp) + EPSILON)[:, :1]
         gate = factor * both[:, :UNITS]
         up = factor * both[:, UNITS:]
         value = gate / (1.0 + jnp.exp(-gate)) * up
-        hidden[smp_rows_of(s), columns(t, UNITS)] = value.astype(jnp.bfloat16)
-        for k in range(1, n_smp):
-            hidden_copy(t, k).start()
-
-    lag = min(2, steps)
-
-    @pl.loop(0, steps)
+        hidden[k, smp_rows_of(s), columns(t, UNITS)] = value.astype(jnp.bfloat16)
+        for m in range(1, n_smp):
+            hidden_copy(i, m).start()
+
+    def gate_up(i):
+        k, t = lax.div(i, steps), lax.rem(i, steps)
+
+        @pl.when(t == 0)
+        def _():
+            prepare(k)
+
+        for copy in weight_copies(i):
+            copy.wait()
+        slot = lax.rem(i, slots)
+        part[i, :, :UNITS] = jnp.dot(
+            scaled[k], gate_buf[slot], preferred_element_type=jnp.float32
+        ).astype(jnp.bfloat16)
+        part[i, :, UNITS:] = jnp.dot(
+            scaled[k], up_buf[slot], preferred_element_type=jnp.float32
+        ).astype(jnp.bfloat16)
+        for m in range(1, n_smp):
+            part_copy(i, m).start()
+
+        @pl.when(i + slots < all_steps)
+        def _():
+            for copy in weight_copies(i + slots):
+                copy.start()
+
+        @pl.when(i < tiles)
+        def _():
+            down_copy(i).start()
+
+    line = Line(n, c, h, buf_a, recv_a, buf_b, from_left, from_right, sa, ra, ss, rl, rr)
+
+    def down(j):
+        k, t = lax.div(j, tiles), lax.rem(j, tiles)
+
+        @pl.when(t == 0)
+        def _():
+            @pl.loop(0, steps)
+            def _(u):
+                for m in range(1, n_smp):
+                    hidden_copy(k * steps + u, m).wait()
+
+        @pl.when(k == 0)
+        def _():
+            down_copy(t).wait()
+
+        line.give(j, jnp.dot(hidden[k], down_buf[t], preferred_element_type=jnp.float32))
+
+    def emit(j):
+        k, t = lax.div(j, tiles), lax.rem(j, tiles)
+        own = pl.ds(pl.multiple_of(k * sub, sub), sub)
+        value = line.finish(j) + state_ref[c, h, own, columns(t, down_tile)].astype(jnp.float32)
+        mixed_ref[own, columns(t, down_tile)] = value.astype(jnp.bfloat16)
+
+    lag = min(2, all_steps)
+    first = steps + lag + 1
+
+    @pl.loop(0, first + (all_tiles + n) * ratio)
+    def _(i):
+        @pl.when(i < all_steps)
+        def _():
+            gate_up(i)
+
+        @pl.when((i >= lag) & (i < all_steps + lag))
+        def _():
+            act(i - lag)
+
+        j = lax.div(i - first, ratio)
+
+        @pl.when((i >= first) & (lax.rem(i - first, ratio) == 0))
+        def _():
+            @pl.when(j < all_tiles)
+            def _():
+                down(j)
+
+            line.step(j)
+
+            @pl.when(j >= n)
+            def _():
+                emit(j - n)
+
+    @pl.loop(0, all_tiles)
     def _(t):
-        for copy in weight_copies(t):
-            copy.wait()
-        slot = lax.rem(t, slots)
-        part[t, :, :UNITS] = jnp.dot(
-            scaled[...], gate_buf[slot], preferred_element_type=jnp.float32
-        ).astype(jnp.bfloat16)
-        part[t, :, UNITS:] = jnp.dot(
-            scaled[...], up_buf[slot], preferred_element_type=jnp.float32
-        ).astype(jnp.bfloat16)
-        for k in range(1, n_smp):
-            part_copy(t, k).start()
-
-        @pl.when(t + slots < steps)
-        def _():
-            for copy in weight_copies(t + slots):
-                copy.start()
-
-        @pl.when(t < tiles)
-        def _():
-            down_copy(t).start()
-
-        @pl.when(t == lag)
-        def _():
-            for k in range(1, n_smp):
-                square_copy(k).wait()
-
-        @pl.when(t >= lag)
-        def _():
-            act(t - lag)
-
-    if steps <= lag:
-        for k in range(1, n_smp):
-            square_copy(k).wait()
-
-    for t in range(steps, tiles):
-        down_copy(t).start()
-
-    @pl.loop(steps - lag, steps)
-    def _(t):
-        act(t)
-
-    @pl.loop(0, steps)
-    def _(t):
-        for k in range(1, n_smp):
-            hidden_copy(t, k).wait()
-
-    scatter = Scatter(n, c, h, buf_a, recv_a, buf_b, recv_b, sa, ra, sb, rb)
-
-    @pl.loop(0, tiles)
-    def _(t):
-        down_copy(t).wait()
-        scatter.give(t, jnp.dot(hidden[...], down_buf[t], preferred_element_type=jnp.float32))
-
-        @pl.when(t >= 1)
-        def _():
-            scatter.middle(t - 1)
-
-    scatter.middle(tiles - 1)
-
-    @pl.loop(0, tiles)
-    def _(t):
-        own = scatter.finish(t) + state_ref[c, h, :, columns(t, TILE)].astype(jnp.float32)
-        mixed_ref[:, columns(t, TILE)] = own.astype(jnp.bfloat16)
+        line.drain(t)
 
 
 def feed_forward(n, n_smp, state, gain, gate, up, down):
     _, _, rows, width = state.shape
-    all_rows = n * 2 * rows
-    smp_rows = all_rows // n_smp
+    sub = SUB if rows % SUB == 0 else rows
+    subsets = rows // sub
+    sub_rows = n * 2 * sub
+    smp_rows = sub_rows // n_smp
     units = gate.shape[1]
-    steps, tiles = units // UNITS, width // TILE
-    slots = min(SLOTS, steps)
+    steps = units // UNITS
+    down_tile = max(DOWN_TILE, width // steps)
+    tiles = width // down_tile
+    all_steps, all_tiles = subsets * steps, subsets * tiles
+    slots = min(SLOTS, all_steps)
     vmem = pl.BlockSpec(memory_space=pltpu.VMEM)
     hbm = pl.BlockSpec(memory_space=pl.ANY)
     dma = pltpu.SemaphoreType.DMA
@@ -726,32 +769,34 @@
         in_specs=[vmem, vmem, hbm, hbm, hbm],
         out_specs=vmem,
         scratch_shapes=[
-            pltpu.VMEM((all_rows, width), bf16),
-            pltpu.VMEM((all_rows, 128), jnp.float32),
-            pltpu.VMEM((n_smp - 1, smp_rows, 128), jnp.float32),
+            pltpu.VMEM((subsets, sub_rows, width), bf16),
+            pltpu.VMEM((subsets, sub_rows, 128), jnp.float32),
+            pltpu.VMEM((subsets, n_smp - 1, smp_rows, 128), jnp.float32),
             pltpu.VMEM((slots, width, UNITS), bf16),
             pltpu.VMEM((slots, width, UNITS), bf16),
-            pltpu.VMEM((tiles, units, TILE), bf16),
-            pltpu.VMEM((steps, all_rows, 2 * UNITS), bf16),
-            pltpu.VMEM((steps, n_smp - 1, smp_rows, 2 * UNITS), bf16),
-            pltpu.VMEM((all_rows, units), bf16),
-            pltpu.VMEM((tiles, 2, n, rows, TILE), bf16),
-            pltpu.VMEM((tiles, n, rows, TILE), bf16),
-            pltpu.VMEM((tiles, n, rows, TILE), bf16),
-            pltpu.VMEM((tiles, n - 1, rows, TILE), bf16),
+            pltpu.VMEM((tiles, units, down_tile), bf16),
+            pltpu.VMEM((all_steps, sub_rows, 2 * UNITS), bf16),
+            pltpu.VMEM((all_steps, n_smp - 1, smp_rows, 2 * UNITS), bf16),
+            pltpu.VMEM((subsets, sub_rows, units), bf16),
+            pltpu.VMEM((all_tiles, 2, n, sub, down_tile), bf16),
+            pltpu.VMEM((all_tiles, n, sub, down_tile), bf16),
+            pltpu.VMEM((all_tiles, n, sub, down_tile), bf16),
+            pltpu.VMEM((all_tiles, n, sub, down_tile), bf16),
+            pltpu.VMEM((all_tiles, n, sub, down_tile), bf16),
             dma((slots,)),
             dma((slots,)),
             dma((tiles,)),
-            dma((n_smp - 1,)),
-            dma((n_smp - 1,)),
-            dma((steps, n_smp - 1)),
-            dma((steps, n_smp - 1)),
-            dma((steps, n_smp - 1)),
-            dma((steps, n_smp - 1)),
-            dma((tiles,)),
-            dma((tiles,)),
-            dma((tiles, n - 1)),
-            dma((tiles, n - 1)),
+            dma((subsets, n_smp - 1)),
+            dma((subsets, n_smp - 1)),
+            dma((all_steps, n_smp - 1)),
+            dma((all_steps, n_smp - 1)),
+            dma((all_steps, n_smp - 1)),
+            dma((all_steps, n_smp - 1)),
+            dma((all_tiles,)),
+            dma((all_tiles,)),
+            dma((all_tiles, n)),
+            dma((all_tiles, n)),
+            dma((all_tiles, n)),
         ],
         compiler_params=pltpu.CompilerParams(
             collective_id=1, has_side_effects=True, vmem_limit_bytes=VMEM_BYTES

time: 179 us -> 174 us (0.972)
  Pallas kernels: 166 us -> 162 us
    pallas_call x1, Pallas kernels: 68.9 us -> 64.2 us  [feed_forward(): pl.pallas_call(functools.partial(ffn_kernel, n, n_smp), out_shape=jax.Sha...]
where the time goes in v1:
time: 174 us; the launch traced here: 173 us
  Pallas kernels  162 us (93%)
  local copies, waits for them, and re-layouts  5.59 us (3%)
  other arithmetic  3.52 us (2%)
  matrix products  2.69 us (2%)
    pallas_call x1, Pallas kernels, project(): pl.pallas_call(functools.partial(proj_kernel, n, n_smp), out_shape=jax.Sh...  85.5 us
    pallas_call x1, Pallas kernels, feed_forward(): pl.pallas_call(functools.partial(ffn_kernel, n, n_smp), out_shape=jax.Sha...  64.2 us
    pallas_call x1, Pallas kernels, suffix_piece(): pl.pallas_call(suffix_kernel, grid=(rows // block,), out_shape=(jax.Shape...  12 us

profile of v1, /device:TPU:0, one launch (start us, length us, event | category | flops | bytes accessed | tf_op | source)
XLA Modules:
  0.0 173.5 jit_solution(1672003611028315392)
XLA Ops:
  0.0 0.0 copy-start
  0.0 0.8 compare_select_fusion
  0.8 0.1 fusion.3
  0.9 0.0 copy-done
  0.9 0.7 gather_fusion
  1.6 0.6 broadcast_select_fusion
  2.2 2.3 %gather_fusion.1 = bf16[32,4096]{1,0:T(8,128)(2,1)S(1)} fusion(bf16[128,4096]{1,0:T(8,128)(2,1)} %bitcast.16, s32[1024]{0:T(1024)S(1)} %pad_clamp_fusion), kind=kCustom, calls=%fused_computation.1 | custom fusion | bytes 524416 | tf_op jit(solution)/shard_map/jit(_take)/gather | solution.py:829
  4.5 0.8 bitcast_select_fusion.queries_ref
  5.3 12.0 %shard_map.109 = (bf16[32,32,128]{2,1,0:T(8,128)(2,1)}, f32[32,32,1]{2,1,0:T(8,128)}) custom-call(s32[32]{0:T(128)} %get-tuple-element.9.lengths_ref, bf16[32,32,128]{2,1,0:T(8,128)(2,1)} %bitcast_select_fusion.queries_ref, bf16[2,32,128,512]{3,2,1,0:T(8,128)(2,1)} %bitcast.18), custom_call_target="tpu_custom_call" | custom-call | tf_op jit(solution)/shard_map/pallas_call | solution.py:58
  17.3 1.2 reduce
  18.6 0.2 fusion
  18.8 0.9 copy.13
  19.6 2.5 %convolution_convert_fusion.suf_ref = bf16[128,4096]{1,0:T(8,128)(2,1)} fusion(bf16[4,8,32,128]{3,2,1,0:T(8,128)(2,1)} %bitcast.23, s32[32]{0:T(128)S(1)} %get-tuple-element.12), kind=kOutput, calls=%fused_computation.2 | convolution fusion | flops 34082816 | bytes 1310848 | tf_op jit(solution)/shard_map/dot_general | solution.py:833
  22.1 85.5 %shard_map.110.state_ref = bf16[4,2,32,4096]{3,2,1,0:T(8,128)(2,1)} custom-call(bf16[128,4096]{1,0:T(8,128)(2,1)} %bitcast.17, bf16[2,1024,512]{2,1,0:T(8,128)(2,1)} %bitcast.20, bf16[128,4096]{1,0:T(8,128)(2,1)} %convolution_convert_fusion.suf_ref, f32[4,128,8]{2,1,0:T(8,128)} %bitcast.22, bf16[1024,4096]{1,0:T(8,128)(2,1)} %bitcast.19, ...), custom_call_target="tpu_custom_call" | custom-call | tf_op jit(solution)/shard_map/pallas_call | solution.py:484
  107.6 0.0 copy-start.1
  107.6 64.2 %shard_map.111 = bf16[32,4096]{1,0:T(8,128)(2,1)} custom-call(bf16[4,2,32,4096]{3,2,1,0:T(8,128)(2,1)} %shard_map.110.state_ref, f32[1,4096]{1,0:T(1,128)} %bitcast.24, bf16[4096,2048]{1,0:T(8,128)(2,1)} %gate_ref.1, bf16[4096,2048]{1,0:T(8,128)(2,1)} %up_ref.1, bf16[2048,4096]{1,0:T(8,128)(2,1)} %down_ref.1), custom_call_target="tpu_custom_call" | custom-call | tf_op jit(solution)/shard_map/pallas_call | solution.py:766
  171.8 1.7 copy.21
  173.5 0.0 copy-done.1
  (2 shorter events, 0.0 us)
Async XLA Ops:
  0.0 0.9 copy-start
  107.6 65.9 %copy-start.1 = (s32[128]{0:T(128)S(1)}, s32[128]{0:T(128)}, u32[]{:S(2)}) copy-start(s32[128]{0:T(128)} %param.14) | copy-start | bytes 1540

commit v2 on v1

--- a/solution.py
+++ b/solution.py
@@ -14,65 +14,6 @@
 
 
 EPSILON = 1e-05
-
-
-def suffix_kernel(lengths_ref, queries_ref, cache_ref, out_ref, lse_ref):
-    block, heads, _ = queries_ref.shape
-    positions_here, width = cache_ref.shape[2:]
-    per_key = heads // (width // HD)
-    first = pl.program_id(0) * block
-    same = (
-        lax.broadcasted_iota(jnp.int32, (heads, width), 0) // per_key
-        == lax.broadcasted_iota(jnp.int32, (heads, width), 1) // HD
-    )
-    positions = lax.broadcasted_iota(jnp.int32, (heads, positions_here), 1)
-    for r in range(block):
-        q = queries_ref[r].astype(jnp.float32)
-        spread = jnp.concatenate([q] * (width // HD), axis=1)
-        spread = jnp.where(same, spread, 0.0).astype(jnp.bfloat16)
-        scores = lax.dot_general(
-            spread, cache_ref[0, r], (((1,), (1,)), ((), ())), preferred_element_type=jnp.float32
-        )
-        scores = jnp.where(positions < lengths_ref[first + r], scores * HD ** (-0.5), -jnp.inf)
-        high = jnp.max(scores, axis=1, keepdims=True)
-        weights = jnp.exp(scores - high)
-        total = jnp.sum(weights, axis=1, keepdims=True)
-        summed = jnp.dot(
-            weights.astype(jnp.bfloat16), cache_ref[1, r], preferred_element_type=jnp.float32
-        )
-        own = jnp.concatenate(
-            [
-                summed[j * per_key : (j + 1) * per_key, j * HD : (j + 1) * HD]
-                for j in range(width // HD)
-            ],
-            axis=0,
-        )
-        out_ref[r] = (own / total).astype(jnp.bfloat16)
-        lse_ref[r] = high + jnp.log(total)
-
-
-def suffix_piece(row_queries, suffix_cache, row_lengths):
-    rows, heads, _ = row_queries.shape
-    block = min(8, rows)
-    _, _, positions_here, width = suffix_cache.shape
-    return pl.pallas_call(
-        suffix_kernel,
-        grid=(rows // block,),
-        out_shape=(
-            jax.ShapeDtypeStruct((rows, heads, HD), jnp.bfloat16),
-            jax.ShapeDtypeStruct((rows, heads, 1), jnp.float32),
-        ),
-        in_specs=[
-            pl.BlockSpec(memory_space=pltpu.SMEM),
-            pl.BlockSpec((block, heads, HD), lambda i: (i, 0, 0)),
-            pl.BlockSpec((2, block, positions_here, width), lambda i: (0, i, 0, 0)),
-        ],
-        out_specs=(
-            pl.BlockSpec((block, heads, HD), lambda i: (i, 0, 0)),
-            pl.BlockSpec((block, heads, 1), lambda i: (i, 0, 0)),
-        ),
-        compiler_params=pltpu.CompilerParams(vmem_limit_bytes=57 * 1024 * 1024),
-    )(row_lengths, row_queries, suffix_cache)
 
 
 MESH = pl.DeviceIdType.MESH
@@ -91,7 +32,7 @@
     )
 
 
-def greet(n, n_smp, c, s, h):
+def announce(n, n_smp, c, s, h):
     barrier = pltpu.get_barrier_semaphore()
     for k in range(1, n):
         pl.semaphore_signal(barrier, inc=1, device_id={"ctx": lax.rem(c + k, n)}, device_id_type=MESH)
@@ -100,7 +41,15 @@
             barrier, inc=1, device_id={"smp": lax.rem(s + k, n_smp)}, device_id_type=MESH
         )
     pl.semaphore_signal(barrier, inc=1, device_id={"head": 1 - h}, device_id_type=MESH)
-    pl.semaphore_wait(barrier, (n - 1) + (n_smp - 1) + 1)
+
+
+def gather_round(n, n_smp):
+    pl.semaphore_wait(pltpu.get_barrier_semaphore(), (n - 1) + (n_smp - 1) + 1)
+
+
+def greet(n, n_smp, c, s, h):
+    announce(n, n_smp, c, s, h)
+    gather_round(n, n_smp)
 
 
 class Line:
@@ -263,16 +212,107 @@
     return pl.ds(pl.multiple_of(t * width, width), width)
 
 
+def suffix_pieces(
+    ids_ref, lengths_ref, q_ref, block_copy, cache, row_q, row_out, row_piece, placed, placed_lse
+):
+    _, rows, positions_here, width = cache.shape
+    samples, features = q_ref.shape
+    keys, _, per_key = placed_lse.shape
+    heads = features // HD
+    block = min(8, rows)
+    ids = ids_ref[...]
+    chosen = (
+        lax.broadcasted_iota(jnp.int32, (samples, ids.shape[1]), 0) == ids
+    ).astype(jnp.float32)
+    picked = chosen.T[:rows]
+    lengths = jnp.sum(picked * lengths_ref[...].astype(jnp.float32), axis=1, keepdims=True)
+    lengths = lengths.astype(jnp.int32)
+    for j in range(keys):
+        lanes = slice(j * per_key * HD, (j + 1) * per_key * HD)
+        own = jnp.dot(
+            picked.astype(jnp.bfloat16), q_ref[:, lanes], preferred_element_type=jnp.float32
+        )
+        for g in range(per_key):
+            row_q[pl.ds(j * per_key + g, rows, stride=heads), :] = own[:, g * HD : (g + 1) * HD]
+
+    same = (
+        lax.broadcasted_iota(jnp.int32, (heads, width), 0) // per_key
+        == lax.broadcasted_iota(jnp.int32, (heads, width), 1) // HD
+    )
+    positions = lax.broadcasted_iota(jnp.int32, (heads, positions_here), 1)
+    lanes_at = lax.broadcasted_iota(jnp.int32, (heads, ids.shape[1]), 1)
+    table = jnp.zeros((heads, ids.shape[1]), jnp.float32)
+    for r0 in range(0, rows, block):
+        block_copy(r0 // block).wait()
+        scores = []
+        for r in range(r0, r0 + block):
+            q = row_q[r * heads : (r + 1) * heads]
+            spread = jnp.concatenate([q] * keys, axis=1)
+            spread = jnp.where(same, spread, 0.0).astype(jnp.bfloat16)
+            one = lax.dot_general(
+                spread, cache[0, r], (((1,), (1,)), ((), ())), preferred_element_type=jnp.float32
+            )
+            live = positions < lengths[r : r + 1]
+            scores.append(jnp.where(live, one * HD ** (-0.5), -jnp.inf))
+        scores = jnp.concatenate(scores, axis=0)
+        high = jnp.max(scores, axis=1, keepdims=True)
+        weights = jnp.exp(scores - high)
+        total = jnp.sum(weights, axis=1, keepdims=True)
+        lse = high + jnp.log(total)
+        weights = weights.astype(jnp.bfloat16)
+        for r in range(r0, r0 + block):
+            part = slice((r - r0) * heads, (r - r0 + 1) * heads)
+            summed = jnp.dot(weights[part], cache[1, r], preferred_element_type=jnp.float32)
+            own = jnp.concatenate(
+                [
+                    summed[j * per_key : (j + 1) * per_key, j * HD : (j + 1) * HD]
+                    for j in range(keys)
+                ],
+                axis=0,
+            )
+            piece = (own / total[part]).astype(jnp.bfloat16)
+            row_out[r * heads : (r + 1) * heads] = piece.astype(jnp.float32)
+            table = jnp.where(lanes_at == r, lse[part], table)
+
+    found = jnp.sum(chosen, axis=1, keepdims=True) > 0.0
+    for k in range(heads):
+        row_piece[:, k * HD : (k + 1) * HD] = row_out[pl.ds(k, rows, stride=heads), :].astype(
+            jnp.bfloat16
+        )
+    to_sample = chosen[:, :rows].astype(jnp.bfloat16)
+    for j in range(keys):
+        lanes = slice(j * per_key * HD, (j + 1) * per_key * HD)
+        placed[:, lanes] = jnp.dot(
+            to_sample, row_piece[:, lanes], preferred_element_type=jnp.float32
+        ).astype(jnp.bfloat16)
+        one = lax.dot_general(
+            chosen,
+            table[j * per_key : (j + 1) * per_key],
+            (((1,), (1,)), ((), ())),
+            precision=lax.Precision.HIGHEST,
+            preferred_element_type=jnp.float32,
+        )
+        placed_lse[j] = jnp.where(found, one, -1e30)
+
+
 def proj_kernel(
     n,
     n_smp,
+    ids_ref,
+    lengths_ref,
     q_ref,
-    kv_ref,
-    suf_ref,
-    suf_lse_ref,
+    kv_hbm,
+    cache_hbm,
     w_ref,
     res_ref,
     state_ref,
+    kv_ref,
+    cache,
+    row_q,
+    row_out,
+    row_piece,
+    suf_ref,
+    suf_lse_ref,
     out_mine,
     lse_mine,
     out_in,
@@ -301,6 +341,8 @@
     gr,
     fs,
     fr,
+    kv_sem,
+    cache_sem,
 ):
     c, s, h = lax.axis_index("ctx"), lax.axis_index("smp"), lax.axis_index("head")
     tiles = w_buf.shape[0]
@@ -308,8 +350,19 @@
     per_dest = out_mine.shape[2] // HD
     dests = per_key // per_dest
     together = 4
-
-    greet(n, n_smp, c, s, h)
+    block = min(8, cache.shape[1])
+
+    def block_copy(i):
+        rows_at = pl.ds(i * block, block)
+        return pltpu.make_async_copy(
+            cache_hbm.at[:, rows_at], cache.at[:, rows_at], cache_sem.at[i]
+        )
+
+    for i in range(cache.shape[1] // block):
+        block_copy(i).start()
+    kv_copy = pltpu.make_async_copy(kv_hbm, kv_ref, kv_sem)
+    kv_copy.start()
+    announce(n, n_smp, c, s, h)
 
     def piece_copies(at, d):
         return (
@@ -323,6 +376,21 @@
     @pl.loop(0, tiles)
     def _(t):
         w_copy(t).start()
+
+    suffix_pieces(
+        ids_ref,
+        lengths_ref,
+        q_ref,
+        block_copy,
+        cache,
+        row_q,
+        row_out,
+        row_piece,
+        suf_ref,
+        suf_lse_ref,
+    )
+    kv_copy.wait()
+    gather_round(n, n_smp)
 
     lanes_at = lax.broadcasted_iota(jnp.int32, (samples, 128), 1)
 
@@ -473,20 +541,30 @@
             pass_copy(t, q).wait()
 
 
-def project(n, n_smp, queries, prefix_cache, suffix_out, suffix_lse, w, residual):
-    keys, samples, per_key = suffix_lse.shape
+def project(n, n_smp, ids, lengths, queries, prefix_cache, suffix_cache, w, residual):
+    samples, heads = queries.shape[0], queries.shape[1] // HD
+    keys = prefix_cache.shape[2] // HD
+    suffix_rows = suffix_cache.shape[1]
     features = queries.shape[1] // n
     rows, width = residual.shape
     tiles = width // TILE
     vmem = pl.BlockSpec(memory_space=pltpu.VMEM)
+    hbm = pl.BlockSpec(memory_space=pl.ANY)
     dma = pltpu.SemaphoreType.DMA
     bf16 = jnp.bfloat16
     return pl.pallas_call(
         functools.partial(proj_kernel, n, n_smp),
         out_shape=jax.ShapeDtypeStruct((n, 2, rows, width), bf16),
-        in_specs=[vmem, vmem, vmem, vmem, pl.BlockSpec(memory_space=pl.ANY), vmem],
+        in_specs=[vmem, vmem, vmem, hbm, hbm, hbm, vmem],
         out_specs=vmem,
         scratch_shapes=[
+            pltpu.VMEM(prefix_cache.shape, bf16),
+            pltpu.VMEM(suffix_cache.shape, bf16),
+            pltpu.VMEM((suffix_rows * heads, HD), jnp.float32),
+            pltpu.VMEM((suffix_rows * heads, HD), jnp.float32),
+            pltpu.VMEM((suffix_rows, heads * HD), bf16),
+            pltpu.VMEM((samples, heads * HD), bf16),
+            pltpu.VMEM((keys, samples, heads // keys), jnp.float32),
             pltpu.VMEM((n, samples, features), bf16),
             pltpu.VMEM((n, 8, samples), jnp.float32),
             pltpu.VMEM((n, samples, features), bf16),
@@ -515,11 +593,13 @@
             dma((tiles, n)),
             dma((tiles, n)),
             dma((tiles, n)),
+            dma,
+            dma((suffix_rows // min(8, suffix_rows),)),
         ],
         compiler_params=pltpu.CompilerParams(
             collective_id=0, has_side_effects=True, vmem_limit_bytes=VMEM_BYTES
         ),
-    )(queries, prefix_cache, suffix_out, suffix_lse, w, residual)
+    )(ids, lengths, queries, prefix_cache, suffix_cache, w, residual)
 
 
 UNITS = 256
@@ -818,35 +898,20 @@
     w_down,
 ):
     group_rows = queries.shape[0]
-    keys_here = prefix_cache.shape[3] // HD
-    heads_local = queries.shape[2] // HD
     n, n_smp = lax.axis_size("ctx"), lax.axis_size("smp")
-    own_queries = queries[:, 0]
     rows_here = suffix_cache.shape[1]
     flat_index = lax.axis_index("ctx") * n_smp + lax.axis_index("smp")
     row_ids = lax.dynamic_slice_in_dim(cache_sample, flat_index * rows_here, rows_here, 0)
-    local_ids = row_ids % group_rows
-    row_queries = jnp.take(own_queries, local_ids, axis=0).reshape(rows_here, heads_local, HD)
-    row_lengths = jnp.take(suffix_length, local_ids, axis=0)
-    suffix_out, suffix_lse = suffix_piece(row_queries, suffix_cache[:, :, :, 0], row_lengths)
-    chosen = local_ids[None, :] == jnp.arange(group_rows, dtype=jnp.int32)[:, None]
-    placed_out = jnp.dot(
-        chosen.astype(jnp.bfloat16),
-        suffix_out.reshape(rows_here, -1),
-        preferred_element_type=jnp.float32,
-    ).astype(jnp.bfloat16)
-    placed_lse = jnp.dot(
-        chosen.astype(jnp.float32), suffix_lse[:, :, 0], precision=lax.Precision.HIGHEST
-    )
-    placed_lse = jnp.where(jnp.any(chosen, axis=1)[:, None], placed_lse, -1e30)
-    placed_lse = placed_lse.reshape(group_rows, keys_here, -1).transpose(1, 0, 2)
+    local_ids = row_ids - lax.axis_index("smp") * group_rows
+    local_ids = jnp.pad(local_ids, (0, 128 - rows_here), constant_values=-1)
     state = project(
         n,
         n_smp,
-        own_queries,
+        local_ids[None, :],
+        suffix_length[None, :],
+        queries[:, 0],
         prefix_cache[:, :, 0],
-        placed_out,
-        placed_lse,
+        suffix_cache[:, :, :, 0],
         w_out[0],
         residual,
     )

time: 174 us -> 155 us (0.89)
  Pallas kernels: 162 us -> 152 us
  local copies, waits for them, and re-layouts: 5.59 us -> 2.18 us
  other arithmetic: 3.52 us -> 0.75 us
  matrix products: 2.69 us -> 0 us
    pallas_call x1 -> x0, Pallas kernels: 12 us -> none  [suffix_piece(): pl.pallas_call(suffix_kernel, grid=(rows // block,), out_shape=(jax.Shape...]
    gather x2 -> x0, local copies, waits for them, and re-layouts: 3.01 us -> none  [the longest x1 2.31 us: on_device(): jnp.take(own_queries, local_ids, axis=0).reshape(rows_here, heads_local, HD)]
    dot_general x2 -> x0, matrix products: 2.69 us -> none  [the longest x1 2.48 us: on_device(): jnp.dot(chosen.astype(jnp.bfloat16), suffix_out.reshape(rows_here, -1), p...]
    pallas_call x1, Pallas kernels: 85.5 us -> 88 us  [project(): pl.pallas_call(functools.partial(proj_kernel, n, n_smp), out_shape=jax.Sh...]
    select_n x3 -> x0, other arithmetic: 2.17 us -> none  [the longest x2 1.36 us: on_device(): row_lengths = jnp.take(suffix_length, local_ids, axis=0)]
where the time goes in v2:
time: 155 us
  Pallas kernels  152 us (98%)
  local copies, waits for them, and re-layouts  2.18 us (1%)
    pallas_call x1, Pallas kernels, project(): pl.pallas_call(functools.partial(proj_kernel, n, n_smp), out_shape=jax.Sh...  88 us
    pallas_call x1, Pallas kernels, feed_forward(): pl.pallas_call(functools.partial(ffn_kernel, n, n_smp), out_shape=jax.Sha...  64.1 us

profile of v2, /device:TPU:0, one launch (start us, length us, event | category | flops | bytes accessed | tf_op | source)
XLA Modules:
  0.0 155.1 jit_solution(5270547371533917607)
XLA Ops:
  0.0 0.8 dynamic-slice_subtract_fusion
  0.8 0.5 pad_bitcast_fusion.ids_ref
  1.3 88.0 %shard_map.109.state_ref = bf16[4,2,32,4096]{3,2,1,0:T(8,128)(2,1)} custom-call(s32[1,128]{1,0:T(1,128)} %pad_bitcast_fusion.ids_ref, s32[1,128]{1,0:T(1,128)} %bitcast.13, bf16[128,4096]{1,0:T(8,128)(2,1)} %bitcast.11, bf16[2,1024,512]{2,1,0:T(8,128)(2,1)} %bitcast.10, bf16[2,32,128,512]{3,2,1,0:T(8,128)(2,1)} %bitcast.8, bf16[1024,4096]{1,0:T(8,128)(2,1)} %bitcast.9, ...), custom_call_target="tpu_custom_call" | custom-call | tf_op jit(solution)/shard_map/pallas_call | solution.py:555
  89.3 64.1 %shard_map.110 = bf16[32,4096]{1,0:T(8,128)(2,1)} custom-call(bf16[4,2,32,4096]{3,2,1,0:T(8,128)(2,1)} %shard_map.109.state_ref, f32[1,4096]{1,0:T(1,128)} %bitcast.12, bf16[4096,2048]{1,0:T(8,128)(2,1)} %gate_ref.1, bf16[4096,2048]{1,0:T(8,128)(2,1)} %up_ref.1, bf16[2048,4096]{1,0:T(8,128)(2,1)} %down_ref.1), custom_call_target="tpu_custom_call" | custom-call | tf_op jit(solution)/shard_map/pallas_call | solution.py:846
  153.4 1.7 %copy.13 = bf16[32,4096]{1,0:T(8,128)(2,1)} copy(bf16[32,4096]{1,0:T(8,128)(2,1)} %shard_map.110) | data formatting | bytes 524288

commit v3 on v2

v3 whole, which is shorter than its diff:
```python
import functools
import types

import jax
import jax.numpy as jnp
from jax import lax
from jax.experimental import pallas as pl
from jax.experimental.pallas import tpu as pltpu
from jax.sharding import PartitionSpec as P

D = 8192
QUERY_HEADS = 64
KEY_VALUE_HEADS = 8
HD = 128


EPSILON = 1e-05


MESH = pl.DeviceIdType.MESH
TILE = 1024
UNITS = 256
SLOTS = 3
SUB = 16
VMEM_BYTES = 67043328


def remote(src, dst, send_sem, recv_sem, where):
    return pltpu.make_async_remote_copy(
        src_ref=src,
        dst_ref=dst,
        send_sem=send_sem,
        recv_sem=recv_sem,
        device_id=where,
        device_id_type=MESH,
    )


def announce(n, n_smp, c, s, h):
    barrier = pltpu.get_barrier_semaphore()
    for k in range(1, n):
        pl.semaphore_signal(barrier, inc=1, device_id={"ctx": lax.rem(c + k, n)}, device_id_type=MESH)
    for k in range(1, n_smp):
        pl.semaphore_signal(
            barrier, inc=1, device_id={"smp": lax.rem(s + k, n_smp)}, device_id_type=MESH
        )
    pl.semaphore_signal(barrier, inc=1, device_id={"head": 1 - h}, device_id_type=MESH)


def gather_round(n, n_smp):
    pl.semaphore_wait(pltpu.get_barrier_semaphore(), (n - 1) + (n_smp - 1) + 1)


class Line:
    def __init__(self, n, c, h, buf_a, recv_a, buf_b, from_left, from_right, sa, ra, ss, rl, rr):
        self.n, self.c, self.h = n, c, h
        self.buf_a, self.recv_a, self.buf_b = buf_a, recv_a, buf_b
        self.from_left, self.from_right = from_left, from_right
        self.sa, self.ra, self.ss, self.rl, self.rr = sa, ra, ss, rl, rr
        self.tiles = buf_a.shape[0]

        @pl.when(c == 0)
        def _():
            from_left[:, 0] = jnp.zeros(from_left.shape[:1] + from_left.shape[2:], from_left.dtype)

        @pl.when(c == n - 1)
        def _():
            from_right[:, n - 1] = jnp.zeros(
                from_right.shape[:1] + from_right.shape[2:], from_right.dtype
            )

    def pair_copy(self, t):
        return remote(
            self.buf_a.at[t, 1 - self.h],
            self.recv_a.at[t],
            self.sa.at[t],
            self.ra.at[t],
            {"head": 1 - self.h},
        )

    def to_right(self, t, d):
        return remote(
            self.buf_b.at[t, d],
            self.from_left.at[t, d],
            self.ss.at[t, d],
            self.rl.at[t, d],
            {"ctx": lax.rem(self.c + 1, self.n)},
        )

    def to_left(self, t, d):
        return remote(
            self.buf_b.at[t, d],
            self.from_right.at[t, d],
            self.ss.at[t, d],
            self.rr.at[t, d],
            {"ctx": lax.rem(self.c + self.n - 1, self.n)},
        )

    def give(self, t, value):
        _, _, n, rows, width = self.buf_a.shape
        parts = value.reshape(n, 2, rows, width).astype(jnp.bfloat16)
        self.buf_a[t, 0] = parts[:, 0]
        self.buf_a[t, 1] = parts[:, 1]
        self.pair_copy(t).start()

    def middle(self, t):
        self.pair_copy(t).wait()
        both = self.buf_a[t, self.h].astype(jnp.float32) + self.recv_a[t].astype(jnp.float32)
        self.buf_b[t] = both.astype(jnp.bfloat16)

    def hop(self, t, inside, d, copy_of, arrived, first):
        @pl.when(inside & (t >= 0) & (t < self.tiles))
        def _():
            @pl.when(jnp.logical_not(first))
            def _():
                copy_of(t, d).wait_recv()
                both = self.buf_b[t, d].astype(jnp.float32) + arrived[t, d].astype(jnp.float32)
                self.buf_b[t, d] = both.astype(jnp.bfloat16)

            copy_of(t, d).start()

    def step(self, i):
        n, c = self.n, self.c

        @pl.when((i >= 1) & (i <= self.tiles))
        def _():
            self.middle(i - 1)

        for e in range(n - 1):
            right, left = n - 1 - e, e
            self.hop(i - 1 - c, right > c, right, self.to_right, self.from_left, c == 0)
            self.hop(i - n + c, left < c, left, self.to_left, self.from_right, c == n - 1)

    def finish(self, t):
        n, c = self.n, self.c

        @pl.when(c > 0)
        def _():
            self.to_right(t, c).wait_recv()

        @pl.when(c < n - 1)
        def _():
            self.to_left(t, c).wait_recv()

        return (
            self.buf_b[t, c].astype(jnp.float32)
            + self.from_left[t, c].astype(jnp.float32)
            + self.from_right[t, c].astype(jnp.float32)
        )

    def drain(self, t):
        for d in range(self.n):

            @pl.when(d > self.c)
            def _():
                self.to_right(t, d).wait_send()

            @pl.when(d < self.c)
            def _():
                self.to_left(t, d).wait_send()


def columns(t, width):
    return pl.ds(pl.multiple_of(t * width, width), width)


def suffix_pieces(
    ids_ref, lengths_ref, q_ref, block_copy, cache, row_q, row_out, row_piece, placed, placed_lse
):
    _, rows, positions_here, width = cache.shape
    samples, features = q_ref.shape
    keys, _, per_key = placed_lse.shape
    heads = features // HD
    block = min(8, rows)
    ids = ids_ref[...]
    chosen = (
        lax.broadcasted_iota(jnp.int32, (samples, ids.shape[1]), 0) == ids
    ).astype(jnp.float32)
    picked = chosen.T[:rows]
    lengths = jnp.sum(picked * lengths_ref[...].astype(jnp.float32), axis=1, keepdims=True)
    lengths = lengths.astype(jnp.int32)
    for j in range(keys):
        lanes = slice(j * per_key * HD, (j + 1) * per_key * HD)
        own = jnp.dot(
            picked.astype(jnp.bfloat16), q_ref[:, lanes], preferred_element_type=jnp.float32
        )
        for g in range(per_key):
            row_q[pl.ds(j * per_key + g, rows, stride=heads), :] = own[:, g * HD : (g + 1) * HD]

    same = (
        lax.broadcasted_iota(jnp.int32, (heads, width), 0) // per_key
        == lax.broadcasted_iota(jnp.int32, (heads, width), 1) // HD
    )
    positions = lax.broadcasted_iota(jnp.int32, (heads, positions_here), 1)
    lanes_at = lax.broadcasted_iota(jnp.int32, (heads, ids.shape[1]), 1)
    table = jnp.zeros((heads, ids.shape[1]), jnp.float32)
    for r0 in range(0, rows, block):
        block_copy(r0 // block).wait()
        scores = []
        for r in range(r0, r0 + block):
            q = row_q[r * heads : (r + 1) * heads]
            spread = jnp.concatenate([q] * keys, axis=1)
            spread = jnp.where(same, spread, 0.0).astype(jnp.bfloat16)
            one = lax.dot_general(
                spread, cache[0, r], (((1,), (1,)), ((), ())), preferred_element_type=jnp.float32
            )
            live = positions < lengths[r : r + 1]
            scores.append(jnp.where(live, one * HD ** (-0.5), -jnp.inf))
        scores = jnp.concatenate(scores, axis=0)
        high = jnp.max(scores, axis=1, keepdims=True)
        weights = jnp.exp(scores - high)
        total = jnp.sum(weights, axis=1, keepdims=True)
        lse = high + jnp.log(total)
        weights = weights.astype(jnp.bfloat16)
        for r in range(r0, r0 + block):
            part = slice((r - r0) * heads, (r - r0 + 1) * heads)
            summed = jnp.dot(weights[part], cache[1, r], preferred_element_type=jnp.float32)
            own = jnp.concatenate(
                [
                    summed[j * per_key : (j + 1) * per_key, j * HD : (j + 1) * HD]
                    for j in range(keys)
                ],
                axis=0,
            )
            piece = (own / total[part]).astype(jnp.bfloat16)
            row_out[r * heads : (r + 1) * heads] = piece.astype(jnp.float32)
            table = jnp.where(lanes_at == r, lse[part], table)

    found = jnp.sum(chosen, axis=1, keepdims=True) > 0.0
    for k in range(heads):
        row_piece[:, k * HD : (k + 1) * HD] = row_out[pl.ds(k, rows, stride=heads), :].astype(
            jnp.bfloat16
        )
    to_sample = chosen[:, :rows].astype(jnp.bfloat16)
    for j in range(keys):
        lanes = slice(j * per_key * HD, (j + 1) * per_key * HD)
        placed[:, lanes] = jnp.dot(
            to_sample, row_piece[:, lanes], preferred_element_type=jnp.float32
        ).astype(jnp.bfloat16)
        one = lax.dot_general(
            chosen,
            table[j * per_key : (j + 1) * per_key],
            (((1,), (1,)), ((), ())),
            precision=lax.Precision.HIGHEST,
            preferred_element_type=jnp.float32,
        )
        placed_lse[j] = jnp.where(found, one, -1e30)


def layer_kernel(n, n_smp, names, *refs):
    r = types.SimpleNamespace(**dict(zip(names, refs, strict=True)))
    c, s, h = lax.axis_index("ctx"), lax.axis_index("smp"), lax.axis_index("head")
    q_ref, kv_ref, suf_ref, suf_lse_ref = r.q, r.kv, r.placed, r.placed_lse
    out_mine, lse_mine, out_in, lse_in, attn = r.out_mine, r.lse_mine, r.out_in, r.lse_in, r.attn
    os, orr, ls, lr, xs, xr = r.os, r.orr, r.ls, r.lr, r.xs, r.xr
    state = r.state
    keys, samples, per_key = suf_lse_ref.shape
    per_dest = out_mine.shape[2] // HD
    dests = per_key // per_dest
    together = 4
    slots, width, _ = r.gate_buf.shape
    tiles, units, tile = r.down_buf.shape
    subsets, sub_rows, _ = r.scaled.shape
    sub = state.shape[2] // subsets
    smp_rows = sub_rows // n_smp
    steps = units // UNITS
    all_steps, all_tiles = subsets * steps, subsets * tiles
    ratio = max(1, steps // tiles)
    w_rows = r.w_hbm.shape[0]
    per_slot = units // w_rows
    w_slots = -(-tiles // per_slot)
    block = min(8, r.cache.shape[1])

    def block_copy(i):
        rows_at = pl.ds(i * block, block)
        return pltpu.make_async_copy(
            r.cache_hbm.at[:, rows_at], r.cache.at[:, rows_at], r.cache_sem.at[i]
        )

    def w_block(t):
        first_row = pl.multiple_of(lax.rem(t, per_slot) * w_rows, w_rows)
        return r.down_buf.at[lax.div(t, per_slot), pl.ds(first_row, w_rows)]

    def w_copy(t):
        return pltpu.make_async_copy(r.w_hbm.at[:, columns(t, tile)], w_block(t), r.w_sem.at[t])

    def weight_copies(i):
        slot, t = lax.rem(i, slots), lax.rem(i, steps)
        return (
            pltpu.make_async_copy(
                r.gate_hbm.at[:, columns(t, UNITS)], r.gate_buf.at[slot], r.g_sem.at[slot]
            ),
            pltpu.make_async_copy(
                r.up_hbm.at[:, columns(t, UNITS)], r.up_buf.at[slot], r.u_sem.at[slot]
            ),
        )

    def down_copy(t):
        return pltpu.make_async_copy(
            r.down_hbm.at[:, columns(t, tile)], r.down_buf.at[t], r.d_sem.at[t]
        )

    for i in range(r.cache.shape[1] // block):
        block_copy(i).start()
    kv_copy = pltpu.make_async_copy(r.kv_hbm, kv_ref, r.kv_sem)
    kv_copy.start()
    announce(n, n_smp, c, s, h)

    def piece_copies(at, d):
        return (
            remote(out_mine.at[d], out_in.at[at], os.at[d], orr.at[at], {"ctx": d}),
            remote(lse_mine.at[d], lse_in.at[at], ls.at[d], lr.at[at], {"ctx": d}),
        )

    suffix_pieces(
        r.ids,
        r.lengths,
        q_ref,
        block_copy,
        r.cache,
        r.row_q,
        r.row_out,
        r.row_piece,
        suf_ref,
        suf_lse_ref,
    )
    kv_copy.wait()

    @pl.loop(0, tiles)
    def _(t):
        w_copy(t).start()

    @pl.loop(0, min(slots, all_steps))
    def _(t):
        for copy in weight_copies(t):
            copy.start()

    for t in range(w_slots, tiles):
        down_copy(t).start()
    gather_round(n, n_smp)

    lanes_at = lax.broadcasted_iota(jnp.int32, (samples, 128), 1)

    @pl.loop(0, keys)
    def _(i):
        j = lax.rem(lax.div(c, dests) + 1 + i, keys)
        key = kv_ref[0, :, columns(j, HD)]
        value = kv_ref[1, :, columns(j, HD)]
        own = q_ref[:, columns(j, per_key * HD)]
        placed = suf_ref[:, columns(j, per_key * HD)]
        placed_lse = suf_lse_ref[j]
        tables = [jnp.zeros((samples, 128), jnp.float32) for _ in range(dests)]
        for g0 in range(0, per_key, together):
            rows = jnp.concatenate(
                [own[:, g * HD : (g + 1) * HD] for g in range(g0, g0 + together)], axis=0
            )
            scores = lax.dot_general(
                rows, key, (((1,), (1,)), ((), ())), preferred_element_type=jnp.float32
            ) * HD ** (-0.5)
            high = jnp.max(scores, axis=1, keepdims=True)
            weights = jnp.exp(scores - high)
            total = jnp.sum(weights, axis=1, keepdims=True)
            summed = (
                jnp.dot(weights.astype(jnp.bfloat16), value, preferred_element_type=jnp.float32)
                / total
            )
            lse = high + jnp.log(total)
            for g in range(g0, g0 + together):
                part = slice((g - g0) * samples, (g - g0 + 1) * samples)
                own_lse, other_lse = lse[part], placed_lse[:, g : g + 1]
                top = jnp.maximum(own_lse, other_lse)
                own_weight = jnp.exp(own_lse - top)
                other_weight = jnp.exp(other_lse - top)
                both = own_weight + other_weight
                merged = (
                    own_weight * summed[part]
                    + other_weight * placed[:, g * HD : (g + 1) * HD].astype(jnp.float32)
                ) / both
                at = g % per_dest
                out_mine[j * dests + g // per_dest, :, at * HD : (at + 1) * HD] = merged.astype(
                    jnp.bfloat16
                )
                q = g // per_dest
                tables[q] = jnp.where(lanes_at == at, top + jnp.log(both), tables[q])
        for q in range(dests):
            d = j * dests + q
            lse_mine[d] = tables[q].T[:8]

            @pl.when(d != c)
            def _():
                for copy in piece_copies(c, d):
                    copy.start()

    for k in range(1, n):
        d = lax.rem(c + k, n)
        for copy in piece_copies(d, d):
            copy.wait_recv()
    for k in range(1, n):
        d = lax.rem(c + k, n)
        for copy in piece_copies(c, d):
            copy.wait_send()

    lses = [lse_mine[c]] + [lse_in[lax.rem(c + k, n)] for k in range(1, n)]
    peak = functools.reduce(jnp.maximum, lses)
    scales = [jnp.exp(value - peak) for value in lses]
    denom = functools.reduce(jnp.add, scales)
    blank = jnp.zeros((120, samples), jnp.float32)
    scales = [jnp.concatenate([value / denom, blank], axis=0).T for value in scales]
    for j in range(per_dest):
        lanes = slice(j * HD, (j + 1) * HD)
        total = scales[0][:, j : j + 1] * out_mine[c, :, lanes].astype(jnp.float32)
        for k in range(1, n):
            piece = out_in[lax.rem(c + k, n), :, lanes].astype(jnp.float32)
            total = total + scales[k][:, j : j + 1] * piece
        attn[s, :, lanes] = total.astype(jnp.bfloat16)

    def attn_copy(k):
        return remote(
            attn.at[s], attn.at[s], xs.at[k - 1], xr.at[k - 1], {"smp": lax.rem(s + k, n_smp)}
        )

    for k in range(1, n_smp):
        attn_copy(k).start()
    for k in range(1, n_smp):
        attn_copy(k).wait()

    by_owner = attn[...].reshape(2 * n, subsets, sub, attn.shape[2])
    for k in range(subsets):
        r.attn_rows[k] = by_owner[:, k].reshape(sub_rows, attn.shape[2])

    line = Line(
        n,
        c,
        h,
        r.buf_a,
        r.recv_a,
        r.buf_b,
        r.from_left,
        r.from_right,
        r.sa,
        r.ra,
        r.ss,
        r.rl,
        r.rr,
    )

    def rows_of(k):
        return pl.ds(pl.multiple_of(k * sub, sub), sub)

    def gather_copy(j, q, way, sems):
        k, t = lax.div(j, tiles), lax.rem(j, tiles)
        at = state.at[q, h, rows_of(k), columns(t, tile)]
        return remote(at, at, sems.at[j, q], r.gr.at[j, q], {"ctx": lax.rem(c + way, n)})

    def pass_copy(j, q):
        k, t = lax.div(j, tiles), lax.rem(j, tiles)
        at = state.at[q, h, rows_of(k), columns(t, tile)]
        return remote(at, at, r.fs.at[j, q], r.fr.at[j, q], {"head": 1 - h})

    def spread(j, q, right, left):
        @pl.when(right & (c < n - 1))
        def _():
            gather_copy(j, q, 1, r.gsr).start()

        @pl.when(left & (c > 0))
        def _():
            gather_copy(j, q, n - 1, r.gsl).start()

        pass_copy(j, q).start()

    def project(i):
        @pl.when(i < all_tiles)
        def _():
            k, t = lax.div(i, tiles), lax.rem(i, tiles)

            @pl.when(k == 0)
            def _():
                w_copy(t).wait()

            line.give(
                i, jnp.dot(r.attn_rows[k], w_block(t)[...], preferred_element_type=jnp.float32)
            )

        line.step(i)

        @pl.when((i >= n) & (i < all_tiles + n))
        def _():
            j = i - n
            k, t = lax.div(j, tiles), lax.rem(j, tiles)
            own = line.finish(j) + r.res[rows_of(k), columns(t, tile)].astype(jnp.float32)
            state[c, h, rows_of(k), columns(t, tile)] = own.astype(jnp.bfloat16)
            spread(j, c, c >= 0, c >= 0)

        for q in range(n):
            j = i - n - lax.max(c - q, q - c)

            @pl.when((q != c) & (j >= 0) & (j < all_tiles))
            def _():
                gather_copy(j, q, 1, r.gsr).wait_recv()
                spread(j, q, q < c, q > c)

    def smp_rows_of(p):
        return pl.ds(pl.multiple_of(p * smp_rows, smp_rows), smp_rows)

    def square_copy(k, m):
        p = lax.rem(s + m, n_smp)
        return remote(
            r.squares.at[k, smp_rows_of(p)],
            r.squares_in.at[k, m - 1],
            r.qs.at[k, m - 1],
            r.qr.at[k, m - 1],
            {"smp": p},
        )

    def prepare(k):
        @pl.loop(k * tiles, (k + 1) * tiles)
        def _(j):
            for q in range(n):
                pass_copy(j, q).wait()

        for owner in range(n):
            for core in range(2):
                wide = state[owner, core, rows_of(k)].astype(jnp.float32)
                first_row = (2 * owner + core) * sub
                rows = slice(first_row, first_row + sub)
                r.scaled[k, rows] = (wide * r.gain[...]).astype(jnp.bfloat16)
                sums = jnp.sum(wide * wide, axis=1, keepdims=True)
                r.squares[k, rows] = jnp.broadcast_to(sums, (sub, 128))
        for m in range(1, n_smp):
            square_copy(k, m).start()

    def part_copy(i, m):
        p = lax.rem(s + m, n_smp)
        return remote(
            r.part.at[i, smp_rows_of(p)],
            r.part_in.at[i, m - 1],
            r.ps.at[i, m - 1],
            r.pr.at[i, m - 1],
            {"smp": p},
        )

    def hidden_copy(i, m):
        k, t = lax.div(i, steps), lax.rem(i, steps)
        at = r.hidden.at[k, smp_rows_of(s), columns(t, UNITS)]
        return remote(
            at, at, r.hs.at[i, m - 1], r.hr.at[i, m - 1], {"smp": lax.rem(s + m, n_smp)}
        )

    def act(i):
        k, t = lax.div(i, steps), lax.rem(i, steps)

        @pl.when(t == 0)
        def _():
            for m in range(1, n_smp):
                square_copy(k, m).wait()

        both = r.part[i, smp_rows_of(s)].astype(jnp.float32)
        for m in range(1, n_smp):
            part_copy(i, m).wait()
            both = both + r.part_in[i, m - 1].astype(jnp.float32)
        total = r.squares[k, smp_rows_of(s)]
        for m in range(1, n_smp):
            total = total + r.squares_in[k, m - 1]
        factor = lax.rsqrt(total / (width * n_smp) + EPSILON)[:, :1]
        gate = factor * both[:, :UNITS]
        up = factor * both[:, UNITS:]
        value = gate / (1.0 + jnp.exp(-gate)) * up
        r.hidden[k, smp_rows_of(s), columns(t, UNITS)] = value.astype(jnp.bfloat16)
        for m in range(1, n_smp):
            hidden_copy(i, m).start()

    def gate_up(i):
        k, t = lax.div(i, steps), lax.rem(i, steps)

        @pl.when(t == 0)
        def _():
            prepare(k)

        for copy in weight_copies(i):
            copy.wait()
        slot = lax.rem(i, slots)
        r.part[i, :, :UNITS] = jnp.dot(
            r.scaled[k], r.gate_buf[slot], preferred_element_type=jnp.float32
        ).astype(jnp.bfloat16)
        r.part[i, :, UNITS:] = jnp.dot(
            r.scaled[k], r.up_buf[slot], preferred_element_type=jnp.float32
        ).astype(jnp.bfloat16)
        for m in range(1, n_smp):
            part_copy(i, m).start()

        @pl.when(i + slots < all_steps)
        def _():
            for copy in weight_copies(i + slots):
                copy.start()

    def down(j):
        k, t = lax.div(j, tiles), lax.rem(j, tiles)

        @pl.when(t == 0)
        def _():
            @pl.loop(0, steps)
            def _(u):
                for m in range(1, n_smp):
                    hidden_copy(k * steps + u, m).wait()

        @pl.when(k == 0)
        def _():
            down_copy(t).wait()

        line.drain(j)
        line.give(j, jnp.dot(r.hidden[k], r.down_buf[t], preferred_element_type=jnp.float32))

    def emit(j):
        k, t = lax.div(j, tiles), lax.rem(j, tiles)
        value = line.finish(j) + state[c, h, rows_of(k), columns(t, tile)].astype(jnp.float32)
        r.mixed[rows_of(k), columns(t, tile)] = value.astype(jnp.bfloat16)

    ahead = max(tiles + 2 * n - 1, all_tiles)
    rest = all_tiles + 2 * n - 1 - ahead

    @pl.loop(0, ahead)
    def _(i):
        project(i)

    for t in range(w_slots):
        down_copy(t).start()

    lag = min(2, all_steps)
    first = max(steps + lag + 1, rest)

    @pl.loop(0, first + (all_tiles + n) * ratio)
    def _(i):
        @pl.when(i < all_steps)
        def _():
            gate_up(i)

        @pl.when(i < rest)
        def _():
            project(i + ahead)

        @pl.when((i >= lag) & (i < all_steps + lag))
        def _():
            act(i - lag)

        j = lax.div(i - first, ratio)

        @pl.when((i >= first) & (lax.rem(i - first, ratio) == 0))
        def _():
            @pl.when(j < all_tiles)
            def _():
                down(j)

            line.step(j)

            @pl.when(j >= n)
            def _():
                emit(j - n)

    @pl.loop(0, all_tiles)
    def _(j):
        line.drain(j)
        for q in range(n):

            @pl.when((q <= c) & (c < n - 1))
            def _():
                gather_copy(j, q, 1, r.gsr).wait_send()

            @pl.when((q >= c) & (c > 0))
            def _():
                gather_copy(j, q, n - 1, r.gsl).wait_send()


def layer(
    n, n_smp, ids, lengths, queries, prefix_cache, suffix_cache, w, residual, gain, gate, up, down
):
    samples, heads = queries.shape[0], queries.shape[1] // HD
    keys = prefix_cache.shape[2] // HD
    suffix_rows = suffix_cache.shape[1]
    features = queries.shape[1] // n
    rows, width = residual.shape
    sub = SUB if rows % SUB == 0 else rows
    subsets = rows // sub
    sub_rows = n * 2 * sub
    smp_rows = sub_rows // n_smp
    units = gate.shape[1]
    steps = units // UNITS
    tile = max(TILE, width // steps)
    tiles = width // tile
    all_steps, all_tiles = subsets * steps, subsets * tiles
    slots = min(SLOTS, all_steps)
    vmem = pl.BlockSpec(memory_space=pltpu.VMEM)
    hbm = pl.BlockSpec(memory_space=pl.ANY)
    dma = pltpu.SemaphoreType.DMA
    bf16, f32 = jnp.bfloat16, jnp.float32
    scratch = {
        "kv": pltpu.VMEM(prefix_cache.shape, bf16),
        "cache": pltpu.VMEM(suffix_cache.shape, bf16),
        "row_q": pltpu.VMEM((suffix_rows * heads, HD), f32),
        "row_out": pltpu.VMEM((suffix_rows * heads, HD), f32),
        "row_piece": pltpu.VMEM((suffix_rows, heads * HD), bf16),
        "placed": pltpu.VMEM((samples, heads * HD), bf16),
        "placed_lse": pltpu.VMEM((keys, samples, heads // keys), f32),
        "out_mine": pltpu.VMEM((n, samples, features), bf16),
        "lse_mine": pltpu.VMEM((n, 8, samples), f32),
        "out_in": pltpu.VMEM((n, samples, features), bf16),
        "lse_in": pltpu.VMEM((n, 8, samples), f32),
        "attn": pltpu.VMEM((n_smp, samples, features), bf16),
        "attn_rows": pltpu.VMEM((subsets, sub_rows, features), bf16),
        "state": pltpu.VMEM((n, 2, rows, width), bf16),
        "scaled": pltpu.VMEM((subsets, sub_rows, width), bf16),
        "squares": pltpu.VMEM((subsets, sub_rows, 128), f32),
        "squares_in": pltpu.VMEM((subsets, n_smp - 1, smp_rows, 128), f32),
        "gate_buf": pltpu.VMEM((slots, width, UNITS), bf16),
        "up_buf": pltpu.VMEM((slots, width, UNITS), bf16),
        "down_buf": pltpu.VMEM((tiles, units, tile), bf16),
        "part": pltpu.VMEM((all_steps, sub_rows, 2 * UNITS), bf16),
        "part_in": pltpu.VMEM((all_steps, n_smp - 1, smp_rows, 2 * UNITS), bf16),
        "hidden": pltpu.VMEM((subsets, sub_rows, units), bf16),
        "buf_a": pltpu.VMEM((all_tiles, 2, n, sub, tile), bf16),
        "recv_a": pltpu.VMEM((all_tiles, n, sub, tile), bf16),
        "buf_b": pltpu.VMEM((all_tiles, n, sub, tile), bf16),
        "from_left": pltpu.VMEM((all_tiles, n, sub, tile), bf16),
        "from_right": pltpu.VMEM((all_tiles, n, sub, tile), bf16),
        "kv_sem": dma,
        "cache_sem": dma((suffix_rows // min(8, suffix_rows),)),
        "w_sem": dma((tiles,)),
        "g_sem": dma((slots,)),
        "u_sem": dma((slots,)),
        "d_sem": dma((tiles,)),
    }
    scratch |= {name: dma((n,)) for name in ("os", "orr", "ls", "lr")}
    scratch |= {name: dma((n_smp - 1,)) for name in ("xs", "xr")}
    scratch |= {name: dma((subsets, n_smp - 1)) for name in ("qs", "qr")}
    scratch |= {name: dma((all_steps, n_smp - 1)) for name in ("ps", "pr", "hs", "hr")}
    scratch |= {name: dma((all_tiles,)) for name in ("sa", "ra")}
    scratch |= {
        name: dma((all_tiles, n)) for name in ("ss", "rl", "rr", "gsr", "gsl", "gr", "fs", "fr")
    }
    operands = {
        "ids": (ids, vmem),
        "lengths": (lengths, vmem),
        "q": (queries, vmem),
        "kv_hbm": (prefix_cache, hbm),
        "cache_hbm": (suffix_cache, hbm),
        "w_hbm": (w, hbm),
        "res": (residual, vmem),
        "gain": (gain, vmem),
        "gate_hbm": (gate, hbm),
        "up_hbm": (up, hbm),
        "down_hbm": (down, hbm),
    }
    names = (*operands, "mixed", *scratch)
    return pl.pallas_call(
        functools.partial(layer_kernel, n, n_smp, names),
        out_shape=jax.ShapeDtypeStruct((rows, width), bf16),
        in_specs=[spec for _, spec in operands.values()],
        out_specs=vmem,
        scratch_shapes=list(scratch.values()),
        compiler_params=pltpu.CompilerParams(
            collective_id=0, has_side_effects=True, vmem_limit_bytes=VMEM_BYTES
        ),
    )(*[value for value, _ in operands.values()])


def on_device(
    queries,
    prefix_cache,
    suffix_cache,
    suffix_length,
    cache_sample,
    residual,
    w_out,
    norm_gain,
    gate_matrix,
    w_up,
    w_down,
):
    group_rows = queries.shape[0]
    n, n_smp = lax.axis_size("ctx"), lax.axis_size("smp")
    rows_here = suffix_cache.shape[1]
    flat_index = lax.axis_index("ctx") * n_smp + lax.axis_index("smp")
    row_ids = lax.dynamic_slice_in_dim(cache_sample, flat_index * rows_here, rows_here, 0)
    local_ids = row_ids - lax.axis_index("smp") * group_rows
    local_ids = jnp.pad(local_ids, (0, 128 - rows_here), constant_values=-1)
    return layer(
        n,
        n_smp,
        local_ids[None, :],
        suffix_length[None, :],
        queries[:, 0],
        prefix_cache[:, :, 0],
        suffix_cache[:, :, :, 0],
        w_out[0],
        residual,
        norm_gain[None, :],
        gate_matrix,
        w_up,
        w_down,
    )


def solution(mesh):
    in_specs = (
        P(("group", "smp"), "head", None),
        P(None, ("group", "ctx"), "head", None),
        P(None, ("group", "ctx", "smp"), None, "head", None),
        P(("group", "smp")),
        P("group"),
        P(("group", "ctx", "head"), "smp"),
        P("head", "ctx", "smp"),
        P("smp"),
        P("smp", ("ctx", "head")),
        P("smp", ("ctx", "head")),
        P(("ctx", "head"), "smp"),
    )
    out_specs = P(("group", "ctx", "head"), "smp")
    return jax.shard_map(
        on_device, mesh=mesh, in_specs=in_specs, out_specs=out_specs, check_vma=False
    )
```

time: 155 us -> 142 us (0.916)
  Pallas kernels: 152 us -> 139 us
    pallas_call x2 -> x1, Pallas kernels: 152 us -> 139 us  [layer(): pl.pallas_call(functools.partial(layer_kernel, n, n_smp, names), out_shap...]
where the time goes in v3:
time: 142 us
  Pallas kernels  139 us (98%)
  local copies, waits for them, and re-layouts  2.18 us (2%)
    pallas_call x1, Pallas kernels, layer(): pl.pallas_call(functools.partial(layer_kernel, n, n_smp, names), out_shap...  139 us

profile of v3, /device:TPU:0, one launch (start us, length us, event | category | flops | bytes accessed | tf_op | source)
XLA Modules:
  0.0 141.6 jit_solution(12643021358019722452)
XLA Ops:
  0.0 0.8 dynamic-slice_subtract_fusion
  0.8 0.5 pad_bitcast_fusion.refs_0_
  1.3 138.7 %shard_map.109 = bf16[32,4096]{1,0:T(8,128)(2,1)} custom-call(s32[1,128]{1,0:T(1,128)} %pad_bitcast_fusion.refs_0_, s32[1,128]{1,0:T(1,128)} %bitcast.13, bf16[128,4096]{1,0:T(8,128)(2,1)} %bitcast.11, bf16[2,1024,512]{2,1,0:T(8,128)(2,1)} %bitcast.10, bf16[2,32,128,512]{3,2,1,0:T(8,128)(2,1)} %bitcast.8, bf16[1024,4096]{1,0:T(8,128)(2,1)} %bitcast.9, ...), custom_call_target="tpu_custom_call" | custom-call | tf_op jit(solution)/shard_map/pallas_call | solution.py:753
  140.0 1.7 %copy.13 = bf16[32,4096]{1,0:T(8,128)(2,1)} copy(bf16[32,4096]{1,0:T(8,128)(2,1)} %shard_map.109) | data formatting | bytes 524288

commit v4 on v3

--- a/solution.py
+++ b/solution.py
@@ -109,7 +109,7 @@
         self.buf_b[t] = both.astype(jnp.bfloat16)
 
     def hop(self, t, inside, d, copy_of, arrived, first):
-        @pl.when(inside & (t >= 0) & (t < self.tiles))
+        @pl.when(inside)
         def _():
             @pl.when(jnp.logical_not(first))
             def _():
@@ -119,17 +119,20 @@
 
             copy_of(t, d).start()
 
-    def step(self, i):
+    def step(self, i, tile_at):
         n, c = self.n, self.c
-
-        @pl.when((i >= 1) & (i <= self.tiles))
-        def _():
-            self.middle(i - 1)
-
+        live, t = tile_at(i - 1)
+
+        @pl.when(live)
+        def _():
+            self.middle(t)
+
+        live_r, t_r = tile_at(i - 1 - c)
+        live_l, t_l = tile_at(i - n + c)
         for e in range(n - 1):
             right, left = n - 1 - e, e
-            self.hop(i - 1 - c, right > c, right, self.to_right, self.from_left, c == 0)
-            self.hop(i - n + c, left < c, left, self.to_left, self.from_right, c == n - 1)
+            self.hop(t_r, live_r & (right > c), right, self.to_right, self.from_left, c == 0)
+            self.hop(t_l, live_l & (left < c), left, self.to_left, self.from_right, c == n - 1)
 
     def finish(self, t):
         n, c = self.n, self.c
@@ -165,25 +168,26 @@
 
 
 def suffix_pieces(
-    ids_ref, lengths_ref, q_ref, block_copy, cache, row_q, row_out, row_piece, placed, placed_lse
+    ids_ref, lengths_ref, sub, q_ref, block_copy, cache, row_q, row_out, row_piece, placed, placed_lse
 ):
     _, rows, positions_here, width = cache.shape
-    samples, features = q_ref.shape
-    keys, _, per_key = placed_lse.shape
+    subsets, part_samples, features = q_ref.shape
+    samples = subsets * part_samples
+    keys, _, _, per_key = placed_lse.shape
     heads = features // HD
     block = min(8, rows)
     ids = ids_ref[...]
-    chosen = (
-        lax.broadcasted_iota(jnp.int32, (samples, ids.shape[1]), 0) == ids
-    ).astype(jnp.float32)
-    picked = chosen.T[:rows]
+    sample_at = lax.broadcasted_iota(jnp.int32, (samples, ids.shape[1]), 0)
+    picked = (sample_at == ids).astype(jnp.float32).T[:rows]
     lengths = jnp.sum(picked * lengths_ref[...].astype(jnp.float32), axis=1, keepdims=True)
     lengths = lengths.astype(jnp.int32)
+    spot = ids // sub % subsets * part_samples + ids // (sub * subsets) * sub + ids % sub
+    chosen = (sample_at == jnp.where(ids < 0, -1, spot)).astype(jnp.float32)
+    picked = chosen.T[:rows].astype(jnp.bfloat16)
+    all_q = q_ref[...].reshape(samples, features)
     for j in range(keys):
         lanes = slice(j * per_key * HD, (j + 1) * per_key * HD)
-        own = jnp.dot(
-            picked.astype(jnp.bfloat16), q_ref[:, lanes], preferred_element_type=jnp.float32
-        )
+        own = jnp.dot(picked, all_q[:, lanes], preferred_element_type=jnp.float32)
         for g in range(per_key):
             row_q[pl.ds(j * per_key + g, rows, stride=heads), :] = own[:, g * HD : (g + 1) * HD]
 
@@ -234,9 +238,8 @@
     to_sample = chosen[:, :rows].astype(jnp.bfloat16)
     for j in range(keys):
         lanes = slice(j * per_key * HD, (j + 1) * per_key * HD)
-        placed[:, lanes] = jnp.dot(
-            to_sample, row_piece[:, lanes], preferred_element_type=jnp.float32
-        ).astype(jnp.bfloat16)
+        one = jnp.dot(to_sample, row_piece[:, lanes], preferred_element_type=jnp.float32)
+        placed[:, :, lanes] = one.astype(jnp.bfloat16).reshape(subsets, part_samples, -1)
         one = lax.dot_general(
             chosen,
             table[j * per_key : (j + 1) * per_key],
@@ -244,20 +247,20 @@
             precision=lax.Precision.HIGHEST,
             preferred_element_type=jnp.float32,
         )
-        placed_lse[j] = jnp.where(found, one, -1e30)
+        one = jnp.where(found, one, -1e30)
+        placed_lse[j] = one.reshape(subsets, part_samples, per_key)
 
 
 def layer_kernel(n, n_smp, names, *refs):
     r = types.SimpleNamespace(**dict(zip(names, refs, strict=True)))
     c, s, h = lax.axis_index("ctx"), lax.axis_index("smp"), lax.axis_index("head")
-    q_ref, kv_ref, suf_ref, suf_lse_ref = r.q, r.kv, r.placed, r.placed_lse
-    out_mine, lse_mine, out_in, lse_in, attn = r.out_mine, r.lse_mine, r.out_in, r.lse_in, r.attn
-    os, orr, ls, lr, xs, xr = r.os, r.orr, r.ls, r.lr, r.xs, r.xr
-    state = r.state
-    keys, samples, per_key = suf_lse_ref.shape
-    per_dest = out_mine.shape[2] // HD
+    kv_ref, state = r.kv, r.state
+    out_mine, lse_mine, out_in, lse_in = r.out_mine, r.lse_mine, r.out_in, r.lse_in
+    keys, _, samples, per_key = r.placed_lse.shape
+    per_dest = out_mine.shape[3] // HD
     dests = per_key // per_dest
-    together = 4
+    together = max(1, min(per_key, 512 // samples))
+    stat_lanes = lse_mine.shape[3]
     slots, width, _ = r.gate_buf.shape
     tiles, units, tile = r.down_buf.shape
     subsets, sub_rows, _ = r.scaled.shape
@@ -306,23 +309,22 @@
     kv_copy.start()
     announce(n, n_smp, c, s, h)
 
-    def piece_copies(at, d):
-        return (
-            remote(out_mine.at[d], out_in.at[at], os.at[d], orr.at[at], {"ctx": d}),
-            remote(lse_mine.at[d], lse_in.at[at], ls.at[d], lr.at[at], {"ctx": d}),
-        )
+    by_owner = r.q[...].reshape(samples // sub, subsets, sub, r.q.shape[1])
+    for k in range(subsets):
+        r.q_rows[k] = by_owner[:, k].reshape(samples, r.q.shape[1])
 
     suffix_pieces(
         r.ids,
         r.lengths,
-        q_ref,
+        sub,
+        r.q_rows,
         block_copy,
         r.cache,
         r.row_q,
         r.row_out,
         r.row_piece,
-        suf_ref,
-        suf_lse_ref,
+        r.placed,
+        r.placed_lse,
     )
     kv_copy.wait()
 
@@ -341,14 +343,23 @@
 
     lanes_at = lax.broadcasted_iota(jnp.int32, (samples, 128), 1)
 
-    @pl.loop(0, keys)
-    def _(i):
+    def piece_copies(k, at, d):
+        return (
+            remote(
+                out_mine.at[k, d], out_in.at[k, at], r.os.at[k, d], r.orr.at[k, at], {"ctx": d}
+            ),
+            remote(
+                lse_mine.at[k, d], lse_in.at[k, at], r.ls.at[k, d], r.lr.at[k, at], {"ctx": d}
+            ),
+        )
+
+    def prefix_piece(k, i):
         j = lax.rem(lax.div(c, dests) + 1 + i, keys)
         key = kv_ref[0, :, columns(j, HD)]
         value = kv_ref[1, :, columns(j, HD)]
-        own = q_ref[:, columns(j, per_key * HD)]
-        placed = suf_ref[:, columns(j, per_key * HD)]
-        placed_lse = suf_lse_ref[j]
+        own = r.q_rows[k, :, columns(j, per_key * HD)]
+        placed = r.placed[k, :, columns(j, per_key * HD)]
+        placed_lse = r.placed_lse[j, k]
         tables = [jnp.zeros((samples, 128), jnp.float32) for _ in range(dests)]
         for g0 in range(0, per_key, together):
             rows = jnp.concatenate(
@@ -377,56 +388,77 @@
                     + other_weight * placed[:, g * HD : (g + 1) * HD].astype(jnp.float32)
                 ) / both
                 at = g % per_dest
-                out_mine[j * dests + g // per_dest, :, at * HD : (at + 1) * HD] = merged.astype(
+                out_mine[k, j * dests + g // per_dest, :, at * HD : (at + 1) * HD] = merged.astype(
                     jnp.bfloat16
                 )
                 q = g // per_dest
                 tables[q] = jnp.where(lanes_at == at, top + jnp.log(both), tables[q])
         for q in range(dests):
             d = j * dests + q
-            lse_mine[d] = tables[q].T[:8]
+            table = tables[q]
+            if stat_lanes > samples:
+                rest_of = jnp.zeros((stat_lanes - samples, 128), jnp.float32)
+                table = jnp.concatenate([table, rest_of], axis=0)
+            lse_mine[k, d] = table.T[:8]
 
             @pl.when(d != c)
             def _():
-                for copy in piece_copies(c, d):
+                for copy in piece_copies(k, c, d):
                     copy.start()
 
-    for k in range(1, n):
-        d = lax.rem(c + k, n)
-        for copy in piece_copies(d, d):
-            copy.wait_recv()
-    for k in range(1, n):
-        d = lax.rem(c + k, n)
-        for copy in piece_copies(c, d):
-            copy.wait_send()
-
-    lses = [lse_mine[c]] + [lse_in[lax.rem(c + k, n)] for k in range(1, n)]
-    peak = functools.reduce(jnp.maximum, lses)
-    scales = [jnp.exp(value - peak) for value in lses]
-    denom = functools.reduce(jnp.add, scales)
-    blank = jnp.zeros((120, samples), jnp.float32)
-    scales = [jnp.concatenate([value / denom, blank], axis=0).T for value in scales]
-    for j in range(per_dest):
-        lanes = slice(j * HD, (j + 1) * HD)
-        total = scales[0][:, j : j + 1] * out_mine[c, :, lanes].astype(jnp.float32)
-        for k in range(1, n):
-            piece = out_in[lax.rem(c + k, n), :, lanes].astype(jnp.float32)
-            total = total + scales[k][:, j : j + 1] * piece
-        attn[s, :, lanes] = total.astype(jnp.bfloat16)
-
-    def attn_copy(k):
+    def attn_copy(k, m):
+        at = r.attn_rows.at[k, pl.ds(pl.multiple_of(s * samples, samples), samples)]
         return remote(
-            attn.at[s], attn.at[s], xs.at[k - 1], xr.at[k - 1], {"smp": lax.rem(s + k, n_smp)}
-        )
-
-    for k in range(1, n_smp):
-        attn_copy(k).start()
-    for k in range(1, n_smp):
-        attn_copy(k).wait()
-
-    by_owner = attn[...].reshape(2 * n, subsets, sub, attn.shape[2])
-    for k in range(subsets):
-        r.attn_rows[k] = by_owner[:, k].reshape(sub_rows, attn.shape[2])
+            at, at, r.xs.at[k, m - 1], r.xr.at[k, m - 1], {"smp": lax.rem(s + m, n_smp)}
+        )
+
+    def merge_pieces(k):
+        for m in range(1, n):
+            d = lax.rem(c + m, n)
+            for copy in piece_copies(k, d, d):
+                copy.wait_recv()
+        lses = [lse_mine[k, c]] + [lse_in[k, lax.rem(c + m, n)] for m in range(1, n)]
+        peak = functools.reduce(jnp.maximum, lses)
+        scales = [jnp.exp(value - peak) for value in lses]
+        denom = functools.reduce(jnp.add, scales)
+        blank = jnp.zeros((120, stat_lanes), jnp.float32)
+        scales = [
+            jnp.concatenate([value / denom, blank], axis=0).T[:samples] for value in scales
+        ]
+        for j in range(per_dest):
+            lanes = slice(j * HD, (j + 1) * HD)
+            total = scales[0][:, j : j + 1] * out_mine[k, c, :, lanes].astype(jnp.float32)
+            for m in range(1, n):
+                piece = out_in[k, lax.rem(c + m, n), :, lanes].astype(jnp.float32)
+                total = total + scales[m][:, j : j + 1] * piece
+            at = pl.ds(pl.multiple_of(s * samples, samples), samples)
+            r.attn_rows[k, at, lanes] = total.astype(jnp.bfloat16)
+        for m in range(1, n_smp):
+            attn_copy(k, m).start()
+
+    def finish_attn(k):
+        for m in range(1, n_smp):
+            attn_copy(k, m).wait()
+        for m in range(1, n):
+            d = lax.rem(c + m, n)
+            for copy in piece_copies(k, c, d):
+                copy.wait_send()
+
+    @pl.loop(0, keys)
+    def _(i):
+        prefix_piece(0, i)
+
+    early = keys // 2 if subsets > 1 else 0
+    gap = max(0, steps - tiles) if subsets > 1 else 0
+    period = tiles + gap
+    if subsets > 1:
+
+        @pl.loop(0, early)
+        def _(i):
+            prefix_piece(1, i)
+
+    merge_pieces(0)
+    finish_attn(0)
 
     line = Line(
         n,
@@ -468,36 +500,47 @@
 
         pass_copy(j, q).start()
 
+    def state_tile(i):
+        at = lax.max(i, 0)
+        k, t = lax.div(at, period), lax.rem(at, period)
+        return (i >= 0) & (k < subsets) & (t < tiles), k * tiles + t
+
+    def mixed_tile(i):
+        return (i >= 0) & (i < all_tiles), i
+
     def project(i):
-        @pl.when(i < all_tiles)
-        def _():
-            k, t = lax.div(i, tiles), lax.rem(i, tiles)
+        live, j = state_tile(i)
+
+        @pl.when(live)
+        def _():
+            k, t = lax.div(j, tiles), lax.rem(j, tiles)
 
             @pl.when(k == 0)
             def _():
                 w_copy(t).wait()
 
             line.give(
-                i, jnp.dot(r.attn_rows[k], w_block(t)[...], preferred_element_type=jnp.float32)
+                j, jnp.dot(r.attn_rows[k], w_block(t)[...], preferred_element_type=jnp.float32)
             )
 
-        line.step(i)
-
-        @pl.when((i >= n) & (i < all_tiles + n))
-        def _():
-            j = i - n
+        line.step(i, state_tile)
+        ready, done = state_tile(i - n)
+
+        @pl.when(ready)
+        def _():
+            j = done
             k, t = lax.div(j, tiles), lax.rem(j, tiles)
             own = line.finish(j) + r.res[rows_of(k), columns(t, tile)].astype(jnp.float32)
             state[c, h, rows_of(k), columns(t, tile)] = own.astype(jnp.bfloat16)
             spread(j, c, c >= 0, c >= 0)
 
         for q in range(n):
-            j = i - n - lax.max(c - q, q - c)
-
-            @pl.when((q != c) & (j >= 0) & (j < all_tiles))
-            def _():
-                gather_copy(j, q, 1, r.gsr).wait_recv()
-                spread(j, q, q < c, q > c)
+            here, moved = state_tile(i - n - lax.max(c - q, q - c))
+
+            @pl.when((q != c) & here)
+            def _():
+                gather_copy(moved, q, 1, r.gsr).wait_recv()
+                spread(moved, q, q < c, q > c)
 
     def smp_rows_of(p):
         return pl.ds(pl.multiple_of(p * smp_rows, smp_rows), smp_rows)
@@ -615,15 +658,29 @@
         value = line.finish(j) + state[c, h, rows_of(k), columns(t, tile)].astype(jnp.float32)
         r.mixed[rows_of(k), columns(t, tile)] = value.astype(jnp.bfloat16)
 
-    ahead = max(tiles + 2 * n - 1, all_tiles)
-    rest = all_tiles + 2 * n - 1 - ahead
+    ahead = tiles + 2 * n - 1
+    rest = period * (subsets - 1)
+    free_at = max(0, period * (subsets - 1) + tiles - ahead)
+    merge_at = max(keys - early, period - 2)
 
     @pl.loop(0, ahead)
     def _(i):
+        if subsets > 1:
+
+            @pl.when(i == period)
+            def _():
+                finish_attn(1)
+
         project(i)
-
-    for t in range(w_slots):
-        down_copy(t).start()
+        if subsets > 1:
+
+            @pl.when(i < keys - early)
+            def _():
+                prefix_piece(1, i + early)
+
+            @pl.when(i == merge_at)
+            def _():
+                merge_pieces(1)
 
     lag = min(2, all_steps)
     first = max(steps + lag + 1, rest)
@@ -638,6 +695,11 @@
         def _():
             project(i + ahead)
 
+        @pl.when(i == free_at)
+        def _():
+            for t in range(w_slots):
+                down_copy(t).start()
+
         @pl.when((i >= lag) & (i < all_steps + lag))
         def _():
             act(i - lag)
@@ -650,7 +712,7 @@
             def _():
                 down(j)
 
-            line.step(j)
+            line.step(j, mixed_tile)
 
             @pl.when(j >= n)
             def _():
@@ -680,6 +742,8 @@
     rows, width = residual.shape
     sub = SUB if rows % SUB == 0 else rows
     subsets = rows // sub
+    part_samples = samples // subsets
+    stat_lanes = -(-part_samples // 128) * 128
     sub_rows = n * 2 * sub
     smp_rows = sub_rows // n_smp
     units = gate.shape[1]
@@ -698,13 +762,13 @@
         "row_q": pltpu.VMEM((suffix_rows * heads, HD), f32),
         "row_out": pltpu.VMEM((suffix_rows * heads, HD), f32),
         "row_piece": pltpu.VMEM((suffix_rows, heads * HD), bf16),
-        "placed": pltpu.VMEM((samples, heads * HD), bf16),
-        "placed_lse": pltpu.VMEM((keys, samples, heads // keys), f32),
-        "out_mine": pltpu.VMEM((n, samples, features), bf16),
-        "lse_mine": pltpu.VMEM((n, 8, samples), f32),
-        "out_in": pltpu.VMEM((n, samples, features), bf16),
-        "lse_in": pltpu.VMEM((n, 8, samples), f32),
-        "attn": pltpu.VMEM((n_smp, samples, features), bf16),
+        "q_rows": pltpu.VMEM((subsets, part_samples, heads * HD), bf16),
+        "placed": pltpu.VMEM((subsets, part_samples, heads * HD), bf16),
+        "placed_lse": pltpu.VMEM((keys, subsets, part_samples, heads // keys), f32),
+        "out_mine": pltpu.VMEM((subsets, n, part_samples, features), bf16),
+        "lse_mine": pltpu.VMEM((subsets, n, 8, stat_lanes), f32),
+        "out_in": pltpu.VMEM((subsets, n, part_samples, features), bf16),
+        "lse_in": pltpu.VMEM((subsets, n, 8, stat_lanes), f32),
         "attn_rows": pltpu.VMEM((subsets, sub_rows, features), bf16),
         "state": pltpu.VMEM((n, 2, rows, width), bf16),
         "scaled": pltpu.VMEM((subsets, sub_rows, width), bf16),
@@ -728,9 +792,8 @@
         "u_sem": dma((slots,)),
         "d_sem": dma((tiles,)),
     }
-    scratch |= {name: dma((n,)) for name in ("os", "orr", "ls", "lr")}
-    scratch |= {name: dma((n_smp - 1,)) for name in ("xs", "xr")}
-    scratch |= {name: dma((subsets, n_smp - 1)) for name in ("qs", "qr")}
+    scratch |= {name: dma((subsets, n)) for name in ("os", "orr", "ls", "lr")}
+    scratch |= {name: dma((subsets, n_smp - 1)) for name in ("xs", "xr", "qs", "qr")}
     scratch |= {name: dma((all_steps, n_smp - 1)) for name in ("ps", "pr", "hs", "hr")}
     scratch |= {name: dma((all_tiles,)) for name in ("sa", "ra")}
     scratch |= {

time: 142 us -> 140 us (0.986)
  Pallas kernels: 139 us -> 136 us
    pallas_call x1, Pallas kernels: 139 us -> 136 us  [layer(): pl.pallas_call(functools.partial(layer_kernel, n, n_smp, names), out_shap...]
where the time goes in v4:
time: 140 us; the launch traced here: 139 us
  Pallas kernels  136 us (97%)
  local copies, waits for them, and re-layouts  2.18 us (2%)
    pallas_call x1, Pallas kernels, layer(): pl.pallas_call(functools.partial(layer_kernel, n, n_smp, names), out_shap...  136 us

profile of v4, /device:TPU:0, one launch (start us, length us, event | category | flops | bytes accessed | tf_op | source)
XLA Modules:
  0.0 139.3 jit_solution(12733099612566259369)
XLA Ops:
  0.0 0.8 dynamic-slice_subtract_fusion
  0.8 0.5 pad_bitcast_fusion.refs_0_
  1.3 136.4 %shard_map.109 = bf16[32,4096]{1,0:T(8,128)(2,1)} custom-call(s32[1,128]{1,0:T(1,128)} %pad_bitcast_fusion.refs_0_, s32[1,128]{1,0:T(1,128)} %bitcast.13, bf16[128,4096]{1,0:T(8,128)(2,1)} %bitcast.11, bf16[2,1024,512]{2,1,0:T(8,128)(2,1)} %bitcast.10, bf16[2,32,128,512]{3,2,1,0:T(8,128)(2,1)} %bitcast.8, bf16[1024,4096]{1,0:T(8,128)(2,1)} %bitcast.9, ...), custom_call_target="tpu_custom_call" | custom-call | tf_op jit(solution)/shard_map/pallas_call | solution.py:816
  137.7 1.7 %copy.13 = bf16[32,4096]{1,0:T(8,128)(2,1)} copy(bf16[32,4096]{1,0:T(8,128)(2,1)} %shard_map.109) | data formatting | bytes 524288

commit v5 on v4

--- a/solution.py
+++ b/solution.py
@@ -449,7 +449,7 @@
         prefix_piece(0, i)
 
     early = keys // 2 if subsets > 1 else 0
-    gap = max(0, steps - tiles) if subsets > 1 else 0
+    gap = max(0, steps - tiles) // 2 if subsets > 1 else 0
     period = tiles + gap
     if subsets > 1:
 
@@ -458,6 +458,12 @@
             prefix_piece(1, i)
 
     merge_pieces(0)
+    if subsets > 1:
+
+        @pl.loop(early, keys)
+        def _(i):
+            prefix_piece(1, i)
+
     finish_attn(0)
 
     line = Line(
@@ -661,7 +667,7 @@
     ahead = tiles + 2 * n - 1
     rest = period * (subsets - 1)
     free_at = max(0, period * (subsets - 1) + tiles - ahead)
-    merge_at = max(keys - early, period - 2)
+    merge_at = max(0, period - 2)
 
     @pl.loop(0, ahead)
     def _(i):
@@ -673,10 +679,6 @@
 
         project(i)
         if subsets > 1:
-
-            @pl.when(i < keys - early)
-            def _():
-                prefix_piece(1, i + early)
 
             @pl.when(i == merge_at)
             def _():

time: 140 us -> 133 us (0.950)
  Pallas kernels: 136 us -> 130 us
    pallas_call x1, Pallas kernels: 136 us -> 130 us  [layer(): pl.pallas_call(functools.partial(layer_kernel, n, n_smp, names), out_shap...]
where the time goes in v5:
time: 133 us
  Pallas kernels  130 us (98%)
  local copies, waits for them, and re-layouts  2.18 us (2%)
    pallas_call x1, Pallas kernels, layer(): pl.pallas_call(functools.partial(layer_kernel, n, n_smp, names), out_shap...  130 us

profile of v5, /device:TPU:0, one launch (start us, length us, event | category | flops | bytes accessed | tf_op | source)
XLA Modules:
  0.0 132.9 jit_solution(3475843342814430789)
XLA Ops:
  0.0 0.8 dynamic-slice_subtract_fusion
  0.8 0.5 pad_bitcast_fusion.refs_0_
  1.3 130.0 %shard_map.109 = bf16[32,4096]{1,0:T(8,128)(2,1)} custom-call(s32[1,128]{1,0:T(1,128)} %pad_bitcast_fusion.refs_0_, s32[1,128]{1,0:T(1,128)} %bitcast.13, bf16[128,4096]{1,0:T(8,128)(2,1)} %bitcast.11, bf16[2,1024,512]{2,1,0:T(8,128)(2,1)} %bitcast.10, bf16[2,32,128,512]{3,2,1,0:T(8,128)(2,1)} %bitcast.8, bf16[1024,4096]{1,0:T(8,128)(2,1)} %bitcast.9, ...), custom_call_target="tpu_custom_call" | custom-call | tf_op jit(solution)/shard_map/pallas_call | solution.py:818
  131.2 1.7 %copy.13 = bf16[32,4096]{1,0:T(8,128)(2,1)} copy(bf16[32,4096]{1,0:T(8,128)(2,1)} %shard_map.109) | data formatting | bytes 524288

commit v6 on v5

--- a/solution.py
+++ b/solution.py
@@ -198,9 +198,9 @@
     positions = lax.broadcasted_iota(jnp.int32, (heads, positions_here), 1)
     lanes_at = lax.broadcasted_iota(jnp.int32, (heads, ids.shape[1]), 1)
     table = jnp.zeros((heads, ids.shape[1]), jnp.float32)
+    scores = []
     for r0 in range(0, rows, block):
         block_copy(r0 // block).wait()
-        scores = []
         for r in range(r0, r0 + block):
             q = row_q[r * heads : (r + 1) * heads]
             spread = jnp.concatenate([q] * keys, axis=1)
@@ -210,9 +210,10 @@
             )
             live = positions < lengths[r : r + 1]
             scores.append(jnp.where(live, one * HD ** (-0.5), -jnp.inf))
-        scores = jnp.concatenate(scores, axis=0)
-        high = jnp.max(scores, axis=1, keepdims=True)
-        weights = jnp.exp(scores - high)
+    for r0 in range(0, rows, block):
+        group = jnp.concatenate(scores[r0 : r0 + block], axis=0)
+        high = jnp.max(group, axis=1, keepdims=True)
+        weights = jnp.exp(group - high)
         total = jnp.sum(weights, axis=1, keepdims=True)
         lse = high + jnp.log(total)
         weights = weights.astype(jnp.bfloat16)
@@ -449,7 +450,7 @@
         prefix_piece(0, i)
 
     early = keys // 2 if subsets > 1 else 0
-    gap = max(0, steps - tiles) // 2 if subsets > 1 else 0
+    gap = max(0, steps - tiles) // 4 if subsets > 1 else 0
     period = tiles + gap
     if subsets > 1:
 

time: 133 us -> 132 us (level)
  no operation moved by 1% of the time
where the time goes in v6:
time: 132 us
  Pallas kernels  129 us (98%)
  local copies, waits for them, and re-layouts  2.18 us (2%)
    pallas_call x1, Pallas kernels, layer(): pl.pallas_call(functools.partial(layer_kernel, n, n_smp, names), out_shap...  129 us

profile of v6, /device:TPU:0, one launch (start us, length us, event | category | flops | bytes accessed | tf_op | source)
XLA Modules:
  0.0 132.1 jit_solution(13682789930295486191)
XLA Ops:
  0.0 0.8 dynamic-slice_subtract_fusion
  0.8 0.5 pad_bitcast_fusion.refs_0_
  1.3 129.2 %shard_map.109 = bf16[32,4096]{1,0:T(8,128)(2,1)} custom-call(s32[1,128]{1,0:T(1,128)} %pad_bitcast_fusion.refs_0_, s32[1,128]{1,0:T(1,128)} %bitcast.13, bf16[128,4096]{1,0:T(8,128)(2,1)} %bitcast.11, bf16[2,1024,512]{2,1,0:T(8,128)(2,1)} %bitcast.10, bf16[2,32,128,512]{3,2,1,0:T(8,128)(2,1)} %bitcast.8, bf16[1024,4096]{1,0:T(8,128)(2,1)} %bitcast.9, ...), custom_call_target="tpu_custom_call" | custom-call | tf_op jit(solution)/shard_map/pallas_call | solution.py:819
  130.4 1.7 %copy.13 = bf16[32,4096]{1,0:T(8,128)(2,1)} copy(bf16[32,4096]{1,0:T(8,128)(2,1)} %shard_map.109) | data formatting | bytes 524288

commit v7 on v6

--- a/solution.py
+++ b/solution.py
@@ -176,7 +176,13 @@
     keys, _, _, per_key = placed_lse.shape
     heads = features // HD
     block = min(8, rows)
-    ids = ids_ref[...]
+    all_ids = ids_ref[...]
+    group_rows = all_ids.shape[1]
+    n_smp = lax.axis_size("smp")
+    own_first = (lax.axis_index("ctx") * n_smp + lax.axis_index("smp")) * rows
+    turned = pltpu.roll(all_ids, lax.rem(group_rows - own_first, group_rows), 1)
+    ids = turned[:, :128] - lax.axis_index("smp") * samples
+    ids = jnp.where(lax.broadcasted_iota(jnp.int32, ids.shape, 1) < rows, ids, -1)
     sample_at = lax.broadcasted_iota(jnp.int32, (samples, ids.shape[1]), 0)
     picked = (sample_at == ids).astype(jnp.float32).T[:rows]
     lengths = jnp.sum(picked * lengths_ref[...].astype(jnp.float32), axis=1, keepdims=True)
@@ -841,17 +847,11 @@
     w_up,
     w_down,
 ):
-    group_rows = queries.shape[0]
     n, n_smp = lax.axis_size("ctx"), lax.axis_size("smp")
-    rows_here = suffix_cache.shape[1]
-    flat_index = lax.axis_index("ctx") * n_smp + lax.axis_index("smp")
-    row_ids = lax.dynamic_slice_in_dim(cache_sample, flat_index * rows_here, rows_here, 0)
-    local_ids = row_ids - lax.axis_index("smp") * group_rows
-    local_ids = jnp.pad(local_ids, (0, 128 - rows_here), constant_values=-1)
     return layer(
         n,
         n_smp,
-        local_ids[None, :],
+        cache_sample[None, :],
         suffix_length[None, :],
         queries[:, 0],
         prefix_cache[:, :, 0],

time: 132 us -> 131 us (level)
  no operation moved by 1% of the time
where the time goes in v7:
time: 131 us
  Pallas kernels  129 us (98%)
  local copies, waits for them, and re-layouts  1.67 us (1%)
    pallas_call x1, Pallas kernels, layer(): pl.pallas_call(functools.partial(layer_kernel, n, n_smp, names), out_shap...  129 us

profile of v7, /device:TPU:0, one launch (start us, length us, event | category | flops | bytes accessed | tf_op | source)
XLA Modules:
  0.0 130.8 jit_solution(14114272051894100918)
XLA Ops:
  0.0 129.2 %shard_map.109 = bf16[32,4096]{1,0:T(8,128)(2,1)} custom-call(s32[1,256]{1,0:T(1,128)} %bitcast.12, s32[1,128]{1,0:T(1,128)} %bitcast.13, bf16[128,4096]{1,0:T(8,128)(2,1)} %bitcast.10, bf16[2,1024,512]{2,1,0:T(8,128)(2,1)} %bitcast.9, bf16[2,32,128,512]{3,2,1,0:T(8,128)(2,1)} %bitcast.7, bf16[1024,4096]{1,0:T(8,128)(2,1)} %bitcast.8, ...), custom_call_target="tpu_custom_call" | custom-call | tf_op jit(solution)/shard_map/pallas_call | solution.py:825
  129.2 1.7 %copy.13 = bf16[32,4096]{1,0:T(8,128)(2,1)} copy(bf16[32,4096]{1,0:T(8,128)(2,1)} %shard_map.109) | data formatting | bytes 524288

commit v8 on v7

--- a/solution.py
+++ b/solution.py
@@ -456,7 +456,7 @@
         prefix_piece(0, i)
 
     early = keys // 2 if subsets > 1 else 0
-    gap = max(0, steps - tiles) // 4 if subsets > 1 else 0
+    gap = 0
     period = tiles + gap
     if subsets > 1:
 

time: 131 us -> 132 us (level)
  no operation moved by 1% of the time
where the time goes in v8:
time: 132 us; the launch traced here: 131 us
  Pallas kernels  130 us (98%)
  local copies, waits for them, and re-layouts  1.67 us (1%)
    pallas_call x1, Pallas kernels, layer(): pl.pallas_call(functools.partial(layer_kernel, n, n_smp, names), out_shap...  130 us

profile of v8, /device:TPU:0, one launch (start us, length us, event | category | flops | bytes accessed | tf_op | source)
XLA Modules:
  0.0 131.4 jit_solution(7409859828660298876)
XLA Ops:
  0.0 129.7 %shard_map.109 = bf16[32,4096]{1,0:T(8,128)(2,1)} custom-call(s32[1,256]{1,0:T(1,128)} %bitcast.12, s32[1,128]{1,0:T(1,128)} %bitcast.13, bf16[128,4096]{1,0:T(8,128)(2,1)} %bitcast.10, bf16[2,1024,512]{2,1,0:T(8,128)(2,1)} %bitcast.9, bf16[2,32,128,512]{3,2,1,0:T(8,128)(2,1)} %bitcast.7, bf16[1024,4096]{1,0:T(8,128)(2,1)} %bitcast.8, ...), custom_call_target="tpu_custom_call" | custom-call | tf_op jit(solution)/shard_map/pallas_call | solution.py:825
  129.7 1.7 %copy.13 = bf16[32,4096]{1,0:T(8,128)(2,1)} copy(bf16[32,4096]{1,0:T(8,128)(2,1)} %shard_map.109) | data formatting | bytes 524288
